TPU v7x, 128 devices: a whole 4x4x4 slice. The times are simulated.
128 devices in a mesh: facet: 8 (over y, z_hi), sub: 16 (over z_lo, x, core).
Axes of the slice: x: 4, y: 4, z: 4 (z_hi: 2, z_lo: 2; z = z_hi * 2 + z_lo), core: 2. Of those that a mesh axis runs over, the one named last changes fastest.
Arguments:
- facet_slab: bfloat16 [256, 2, 65536], P('sub', None, 'facet'), may hold values from -6 to 6
- window: float32 [8192], replicated, may hold values from 0.1 to 1
- facet_offsets: int32 [8], replicated, may hold values from 0 to 7, each once
- subgrid_offsets: int32 [8], replicated, may hold values from 0 to 65535
- row_positions: int32 [256], replicated, may hold values from 0 to 65535
- band_offset: int32 [1], replicated, may hold values from 0 to 65535
- mask_extents: int32 [8, 2], replicated, may hold values from 0 to 511
Outputs:
- subgrid_rows: float32 [128, 8, 2, 2048], P('sub', 'facet')
All inputs are finite; a program needn't handle non-finite values.
Results may differ from a plain program's by a relative error of at most 0.0052.
Values may be sent and summed in bfloat16 or wider, within the bound.
A program may use at most 128 MiB of HBM per device.

v0:
```python
import math

import jax
import jax.numpy as jnp
from jax import lax
from jax.sharding import PartitionSpec as P

IMAGE = 65536
SG = 2048
J_DEV = 8


TWO_PI = 2.0 * math.pi


def mul_mod(left, right, modulus):
    right = right % modulus
    high_part = left // 256
    low_part = left % 256
    return (high_part * right % modulus * 256 + low_part * right) % modulus


def cos_sin(index, modulus):
    angle = index.astype(jnp.float32) * (TWO_PI / modulus)
    return (jnp.cos(angle), jnp.sin(angle))


def facet_terms(slab, window, offsets, position, scale):
    num_rows = slab.shape[0]
    facet_width = slab.shape[2]
    sub_count = offsets.shape[0]
    col_block = min(512, facet_width)
    freq = jnp.arange(SG, dtype=jnp.int32)
    inner = jnp.arange(col_block, dtype=jnp.int32)
    base_cos, base_sin = cos_sin(inner[:, None] * freq[None, :] % IMAGE, IMAGE)
    base_sin = -base_sin

    def one_block(block_idx, totals):
        first_col = block_idx * col_block
        cols = first_col + inner
        part_data = lax.dynamic_slice_in_dim(slab, first_col, col_block, 2).astype(jnp.float32)
        weights = lax.dynamic_slice_in_dim(window, first_col, col_block, 0)
        real_in = part_data[:, 0] * weights
        imag_in = part_data[:, 1] * weights
        cos_shift, sin_shift = cos_sin(offsets[:, None] * cols[None, :] % IMAGE, IMAGE)
        sin_shift = -sin_shift
        g_real = real_in[None] * cos_shift[:, None] - imag_in[None] * sin_shift[:, None]
        g_imag = real_in[None] * sin_shift[:, None] + imag_in[None] * cos_shift[:, None]
        g_real = g_real.reshape(sub_count * num_rows, col_block).astype(jnp.bfloat16)
        g_imag = g_imag.reshape(sub_count * num_rows, col_block).astype(jnp.bfloat16)
        phase_cos, phase_sin = cos_sin(first_col * freq % IMAGE, IMAGE)
        phase_sin = -phase_sin
        t_real = (phase_cos[None] * base_cos - phase_sin[None] * base_sin).astype(jnp.bfloat16)
        t_imag = (phase_cos[None] * base_sin + phase_sin[None] * base_cos).astype(jnp.bfloat16)
        f32 = jnp.float32
        acc_real = (
            totals[0]
            + jnp.dot(g_real, t_real, preferred_element_type=f32)
            - jnp.dot(g_imag, t_imag, preferred_element_type=f32)
        )
        acc_imag = (
            totals[1]
            + jnp.dot(g_real, t_imag, preferred_element_type=f32)
            + jnp.dot(g_imag, t_real, preferred_element_type=f32)
        )
        return (acc_real, acc_imag)

    zero_sum = jnp.zeros((sub_count * num_rows, SG), jnp.float32)
    acc_real, acc_imag = lax.fori_loop(0, facet_width // col_block, one_block, (zero_sum, zero_sum))
    acc_real = acc_real.reshape(sub_count, num_rows, SG)
    acc_imag = acc_imag.reshape(sub_count, num_rows, SG)
    ratio = IMAGE // facet_width
    freq_all = (offsets[:, None] + freq[None, :]) % IMAGE
    cos_out, sin_out = cos_sin(position * (freq_all % ratio) % ratio, ratio)
    sin_out = -sin_out
    out_real = (acc_real * cos_out[:, None] - acc_imag * sin_out[:, None]) * scale
    out_imag = (acc_real * sin_out[:, None] + acc_imag * cos_out[:, None]) * scale
    return jnp.stack([out_real, out_imag], axis=2)


def row_terms(stripes, positions, rows_index, band_start, scale):
    shifted = (rows_index + band_start) % IMAGE
    cos_row, sin_row = cos_sin(mul_mod(positions[None, :], shifted[:, None], IMAGE), IMAGE)
    sin_row = -sin_row
    high = lax.Precision.HIGHEST
    first = jnp.einsum("jr,qrck->jqck", cos_row, stripes, precision=high)
    second = jnp.einsum("jr,qrck->jqck", sin_row, stripes, precision=high)
    real_part = first[:, :, 0] - second[:, :, 1]
    imag_part = first[:, :, 1] + second[:, :, 0]
    return jnp.stack([real_part, imag_part], axis=2) * scale


def apply_mask(rows_done, extents, columns):
    keep = (columns[None, :] >= extents[:, 0:1]) & (columns[None, :] < SG - extents[:, 1:2])
    return jnp.where(keep[None, :, None, :], rows_done, jnp.float32(0.0)).astype(jnp.bfloat16)


def finish(masked, base_cos, base_sin):
    freq = jnp.arange(SG, dtype=jnp.int32)
    real_in = masked[:, 0]
    imag_in = masked[:, 1]
    out_block = min(512, SG)
    scale = 1.0 / math.sqrt(SG)
    f32 = jnp.float32
    real_parts = []
    imag_parts = []
    for first_out in range(0, SG, out_block):
        phase_cos, phase_sin = cos_sin(freq * first_out % SG, SG)
        t_cos = (phase_cos[:, None] * base_cos - phase_sin[:, None] * base_sin).astype(jnp.bfloat16)
        t_sin = (phase_cos[:, None] * base_sin + phase_sin[:, None] * base_cos).astype(jnp.bfloat16)
        real_parts.append(
            (
                jnp.dot(real_in, t_cos, preferred_element_type=f32)
                - jnp.dot(imag_in, t_sin, preferred_element_type=f32)
            )
            * scale
        )
        imag_parts.append(
            (
                jnp.dot(real_in, t_sin, preferred_element_type=f32)
                + jnp.dot(imag_in, t_cos, preferred_element_type=f32)
            )
            * scale
        )
    return jnp.stack(
        [jnp.concatenate(real_parts, axis=1), jnp.concatenate(imag_parts, axis=1)], axis=1
    )


def local(
    facet_slab, window, facet_offsets, subgrid_offsets, row_positions, band_offset, mask_extents
):
    facet_count = lax.axis_size("facet")
    facet_idx = lax.axis_index("facet")
    sub_idx = lax.axis_index("sub")
    facet_width = facet_slab.shape[2]
    all_rows = row_positions.shape[0]
    position = lax.dynamic_index_in_dim(facet_offsets, facet_idx, 0, keepdims=False)
    scale_one = 1.0 / math.sqrt(facet_width * facet_count)
    scale_two = 1.0 / math.sqrt(all_rows)
    band_start = band_offset[0]
    contrib = facet_terms(facet_slab, window, subgrid_offsets, position, scale_one)
    stripes = lax.psum_scatter(contrib, "facet", scatter_dimension=3, tiled=True)
    own_rows = sub_idx * J_DEV + jnp.arange(J_DEV, dtype=jnp.int32)
    rows_done = row_terms(
        lax.all_gather(stripes, "sub", axis=1, tiled=True),
        row_positions,
        own_rows,
        band_start,
        scale_two,
    )
    col_width = rows_done.shape[3]
    columns = facet_idx * col_width + jnp.arange(col_width, dtype=jnp.int32)
    masked = apply_mask(rows_done, mask_extents, columns)
    masked = lax.all_to_all(masked, "facet", split_axis=1, concat_axis=3, tiled=True)
    freq = jnp.arange(SG, dtype=jnp.int32)
    inner = jnp.arange(min(512, SG), dtype=jnp.int32)
    base_cos, base_sin = cos_sin(freq[:, None] * inner[None, :] % SG, SG)
    results = [finish(masked[:, 0], base_cos, base_sin)]
    return jnp.stack(results, axis=1)


def solution(mesh):
    return jax.shard_map(
        local,
        mesh=mesh,
        in_specs=(P("sub", None, "facet"), P(), P(), P(), P(), P(), P()),
        out_specs=P("sub", "facet", None, None),
        check_vma=False,
    )
```

profile of v0, /device:TPU:1, one launch (start us, length us, event | category | flops | bytes accessed | tf_op | source)
XLA Modules:
  0.0 1649.5 jit_solution(16251119802106318646)
XLA Ops:
  9.5 1217.2 %while.19 = (s32[]{:T(128)}, f32[128,2048]{1,0:T(8,128)S(1)}, f32[128,2048]{1,0:T(8,128)S(1)}, bf16[16,2,8192]{2,1,0:T(2,128)(2,1)}, f32[8192]{0:T(1024)}, /*ind...) while((s32[]{:T(128)}, f32[128,2048]{1,0:T(8,128)S(1)}, ...), condition=%wide.region_1.2_spmd.clone.clone, body=%wide.region_0.1_spmd.clone.clone.sunk | while | flops 1155656192 | bytes 9758926 | solution.py:69
  12.1 18.4 %convolution_add_fusion.7 = f32[128,2048]{1,0:T(8,128)S(1)} fusion(bf16[128,512]{1,0:T(8,128)(2,1)S(1)} %bitcast.82, f32[2048]{0:T(1024)S(1)} %get-tuple-element.405, f32[2048]{0:T(1024)S(1)} %get-tuple-element.406, f32[128,2048]{1,0:T(8,128)S(1)} %get-tuple-element.420, pred[]{:T(512)S(6)} %compare.58), kind=kOutput, calls=%fused_computation.17.clone.1 | convolution fusion | flops 288882688 | bytes 2244609 | tf_op jit(solution)/shard_map/while/body/eval_jaxpr/dot_general | solution.py:63
  30.5 18.4 %convolution_add_fusion.8 = f32[128,2048]{1,0:T(8,128)S(1)} fusion(f32[128,2048]{1,0:T(8,128)S(1)} %convolution_add_fusion.7, bf16[128,512]{1,0:T(8,128)(2,1)S(1)} %bitcast.80, f32[2048]{0:T(1024)S(1)} %get-tuple-element.405, f32[2048]{0:T(1024)S(1)} %get-tuple-element.406), kind=kOutput, calls=%fused_computation.16.clone.1 | convolution fusion | flops 288620544 | bytes 2244608 | tf_op jit(solution)/shard_map/while/body/eval_jaxpr/dot_general | solution.py:64
  48.8 18.4 %convolution_add_fusion.6 = f32[128,2048]{1,0:T(8,128)S(1)} fusion(bf16[128,512]{1,0:T(8,128)(2,1)S(1)} %bitcast.83, f32[2048]{0:T(1024)S(1)} %get-tuple-element.405, f32[2048]{0:T(1024)S(1)} %get-tuple-element.406, f32[128,2048]{1,0:T(8,128)S(1)} %get-tuple-element.419, pred[]{:T(512)S(6)} %compare.58), kind=kOutput, calls=%fused_computation.19.clone.1 | convolution fusion | flops 288882688 | bytes 2244609 | tf_op jit(solution)/shard_map/while/body/eval_jaxpr/dot_general | solution.py:58
  67.2 18.4 %convolution_subtract_fusion.2 = f32[128,2048]{1,0:T(8,128)S(1)} fusion(f32[128,2048]{1,0:T(8,128)S(1)} %convolution_add_fusion.6, bf16[128,512]{1,0:T(8,128)(2,1)S(1)} %bitcast.81, f32[2048]{0:T(1024)S(1)} %get-tuple-element.405, f32[2048]{0:T(1024)S(1)} %get-tuple-element.406), kind=kOutput, calls=%fused_computation.18.clone.1 | convolution fusion | flops 288620544 | bytes 2244608 | tf_op jit(solution)/shard_map/while/body/eval_jaxpr/dot_general | solution.py:59
  88.2 18.4 %convolution_add_fusion.7 = f32[128,2048]{1,0:T(8,128)S(1)} fusion(bf16[128,512]{1,0:T(8,128)(2,1)S(1)} %bitcast.82, f32[2048]{0:T(1024)S(1)} %get-tuple-element.405, f32[2048]{0:T(1024)S(1)} %get-tuple-element.406, f32[128,2048]{1,0:T(8,128)S(1)} %get-tuple-element.420, pred[]{:T(512)S(6)} %compare.58), kind=kOutput, calls=%fused_computation.17.clone.1 | convolution fusion | flops 288882688 | bytes 2244609 | tf_op jit(solution)/shard_map/while/body/eval_jaxpr/dot_general | solution.py:63
  124.9 18.4 %convolution_add_fusion.6 = f32[128,2048]{1,0:T(8,128)S(1)} fusion(bf16[128,512]{1,0:T(8,128)(2,1)S(1)} %bitcast.83, f32[2048]{0:T(1024)S(1)} %get-tuple-element.405, f32[2048]{0:T(1024)S(1)} %get-tuple-element.406, f32[128,2048]{1,0:T(8,128)S(1)} %get-tuple-element.419, pred[]{:T(512)S(6)} %compare.58), kind=kOutput, calls=%fused_computation.19.clone.1 | convolution fusion | flops 288882688 | bytes 2244609 | tf_op jit(solution)/shard_map/while/body/eval_jaxpr/dot_general | solution.py:58
  143.3 18.4 %convolution_subtract_fusion.2 = f32[128,2048]{1,0:T(8,128)S(1)} fusion(f32[128,2048]{1,0:T(8,128)S(1)} %convolution_add_fusion.6, bf16[128,512]{1,0:T(8,128)(2,1)S(1)} %bitcast.81, f32[2048]{0:T(1024)S(1)} %get-tuple-element.405, f32[2048]{0:T(1024)S(1)} %get-tuple-element.406), kind=kOutput, calls=%fused_computation.18.clone.1 | convolution fusion | flops 288620544 | bytes 2244608 | tf_op jit(solution)/shard_map/while/body/eval_jaxpr/dot_general | solution.py:59
  164.2 18.4 %convolution_add_fusion.7 = f32[128,2048]{1,0:T(8,128)S(1)} fusion(bf16[128,512]{1,0:T(8,128)(2,1)S(1)} %bitcast.82, f32[2048]{0:T(1024)S(1)} %get-tuple-element.405, f32[2048]{0:T(1024)S(1)} %get-tuple-element.406, f32[128,2048]{1,0:T(8,128)S(1)} %get-tuple-element.420, pred[]{:T(512)S(6)} %compare.58), kind=kOutput, calls=%fused_computation.17.clone.1 | convolution fusion | flops 288882688 | bytes 2244609 | tf_op jit(solution)/shard_map/while/body/eval_jaxpr/dot_general | solution.py:63
  182.6 18.4 %convolution_add_fusion.8 = f32[128,2048]{1,0:T(8,128)S(1)} fusion(f32[128,2048]{1,0:T(8,128)S(1)} %convolution_add_fusion.7, bf16[128,512]{1,0:T(8,128)(2,1)S(1)} %bitcast.80, f32[2048]{0:T(1024)S(1)} %get-tuple-element.405, f32[2048]{0:T(1024)S(1)} %get-tuple-element.406), kind=kOutput, calls=%fused_computation.16.clone.1 | convolution fusion | flops 288620544 | bytes 2244608 | tf_op jit(solution)/shard_map/while/body/eval_jaxpr/dot_general | solution.py:64
  201.0 18.4 %convolution_add_fusion.6 = f32[128,2048]{1,0:T(8,128)S(1)} fusion(bf16[128,512]{1,0:T(8,128)(2,1)S(1)} %bitcast.83, f32[2048]{0:T(1024)S(1)} %get-tuple-element.405, f32[2048]{0:T(1024)S(1)} %get-tuple-element.406, f32[128,2048]{1,0:T(8,128)S(1)} %get-tuple-element.419, pred[]{:T(512)S(6)} %compare.58), kind=kOutput, calls=%fused_computation.19.clone.1 | convolution fusion | flops 288882688 | bytes 2244609 | tf_op jit(solution)/shard_map/while/body/eval_jaxpr/dot_general | solution.py:58
  219.3 18.4 %convolution_subtract_fusion.2 = f32[128,2048]{1,0:T(8,128)S(1)} fusion(f32[128,2048]{1,0:T(8,128)S(1)} %convolution_add_fusion.6, bf16[128,512]{1,0:T(8,128)(2,1)S(1)} %bitcast.81, f32[2048]{0:T(1024)S(1)} %get-tuple-element.405, f32[2048]{0:T(1024)S(1)} %get-tuple-element.406), kind=kOutput, calls=%fused_computation.18.clone.1 | convolution fusion | flops 288620544 | bytes 2244608 | tf_op jit(solution)/shard_map/while/body/eval_jaxpr/dot_general | solution.py:59
  240.3 18.4 %convolution_add_fusion.7 = f32[128,2048]{1,0:T(8,128)S(1)} fusion(bf16[128,512]{1,0:T(8,128)(2,1)S(1)} %bitcast.82, f32[2048]{0:T(1024)S(1)} %get-tuple-element.405, f32[2048]{0:T(1024)S(1)} %get-tuple-element.406, f32[128,2048]{1,0:T(8,128)S(1)} %get-tuple-element.420, pred[]{:T(512)S(6)} %compare.58), kind=kOutput, calls=%fused_computation.17.clone.1 | convolution fusion | flops 288882688 | bytes 2244609 | tf_op jit(solution)/shard_map/while/body/eval_jaxpr/dot_general | solution.py:63
  277.1 18.4 %convolution_add_fusion.6 = f32[128,2048]{1,0:T(8,128)S(1)} fusion(bf16[128,512]{1,0:T(8,128)(2,1)S(1)} %bitcast.83, f32[2048]{0:T(1024)S(1)} %get-tuple-element.405, f32[2048]{0:T(1024)S(1)} %get-tuple-element.406, f32[128,2048]{1,0:T(8,128)S(1)} %get-tuple-element.419, pred[]{:T(512)S(6)} %compare.58), kind=kOutput, calls=%fused_computation.19.clone.1 | convolution fusion | flops 288882688 | bytes 2244609 | tf_op jit(solution)/shard_map/while/body/eval_jaxpr/dot_general | solution.py:58
  295.4 18.4 %convolution_subtract_fusion.2 = f32[128,2048]{1,0:T(8,128)S(1)} fusion(f32[128,2048]{1,0:T(8,128)S(1)} %convolution_add_fusion.6, bf16[128,512]{1,0:T(8,128)(2,1)S(1)} %bitcast.81, f32[2048]{0:T(1024)S(1)} %get-tuple-element.405, f32[2048]{0:T(1024)S(1)} %get-tuple-element.406), kind=kOutput, calls=%fused_computation.18.clone.1 | convolution fusion | flops 288620544 | bytes 2244608 | tf_op jit(solution)/shard_map/while/body/eval_jaxpr/dot_general | solution.py:59
  316.4 18.4 %convolution_add_fusion.7 = f32[128,2048]{1,0:T(8,128)S(1)} fusion(bf16[128,512]{1,0:T(8,128)(2,1)S(1)} %bitcast.82, f32[2048]{0:T(1024)S(1)} %get-tuple-element.405, f32[2048]{0:T(1024)S(1)} %get-tuple-element.406, f32[128,2048]{1,0:T(8,128)S(1)} %get-tuple-element.420, pred[]{:T(512)S(6)} %compare.58), kind=kOutput, calls=%fused_computation.17.clone.1 | convolution fusion | flops 288882688 | bytes 2244609 | tf_op jit(solution)/shard_map/while/body/eval_jaxpr/dot_general | solution.py:63
  334.8 18.4 %convolution_add_fusion.8 = f32[128,2048]{1,0:T(8,128)S(1)} fusion(f32[128,2048]{1,0:T(8,128)S(1)} %convolution_add_fusion.7, bf16[128,512]{1,0:T(8,128)(2,1)S(1)} %bitcast.80, f32[2048]{0:T(1024)S(1)} %get-tuple-element.405, f32[2048]{0:T(1024)S(1)} %get-tuple-element.406), kind=kOutput, calls=%fused_computation.16.clone.1 | convolution fusion | flops 288620544 | bytes 2244608 | tf_op jit(solution)/shard_map/while/body/eval_jaxpr/dot_general | solution.py:64
  353.1 18.4 %convolution_add_fusion.6 = f32[128,2048]{1,0:T(8,128)S(1)} fusion(bf16[128,512]{1,0:T(8,128)(2,1)S(1)} %bitcast.83, f32[2048]{0:T(1024)S(1)} %get-tuple-element.405, f32[2048]{0:T(1024)S(1)} %get-tuple-element.406, f32[128,2048]{1,0:T(8,128)S(1)} %get-tuple-element.419, pred[]{:T(512)S(6)} %compare.58), kind=kOutput, calls=%fused_computation.19.clone.1 | convolution fusion | flops 288882688 | bytes 2244609 | tf_op jit(solution)/shard_map/while/body/eval_jaxpr/dot_general | solution.py:58
  371.5 18.4 %convolution_subtract_fusion.2 = f32[128,2048]{1,0:T(8,128)S(1)} fusion(f32[128,2048]{1,0:T(8,128)S(1)} %convolution_add_fusion.6, bf16[128,512]{1,0:T(8,128)(2,1)S(1)} %bitcast.81, f32[2048]{0:T(1024)S(1)} %get-tuple-element.405, f32[2048]{0:T(1024)S(1)} %get-tuple-element.406), kind=kOutput, calls=%fused_computation.18.clone.1 | convolution fusion | flops 288620544 | bytes 2244608 | tf_op jit(solution)/shard_map/while/body/eval_jaxpr/dot_general | solution.py:59
  392.5 18.4 %convolution_add_fusion.7 = f32[128,2048]{1,0:T(8,128)S(1)} fusion(bf16[128,512]{1,0:T(8,128)(2,1)S(1)} %bitcast.82, f32[2048]{0:T(1024)S(1)} %get-tuple-element.405, f32[2048]{0:T(1024)S(1)} %get-tuple-element.406, f32[128,2048]{1,0:T(8,128)S(1)} %get-tuple-element.420, pred[]{:T(512)S(6)} %compare.58), kind=kOutput, calls=%fused_computation.17.clone.1 | convolution fusion | flops 288882688 | bytes 2244609 | tf_op jit(solution)/shard_map/while/body/eval_jaxpr/dot_general | solution.py:63
  410.8 18.4 %convolution_add_fusion.8 = f32[128,2048]{1,0:T(8,128)S(1)} fusion(f32[128,2048]{1,0:T(8,128)S(1)} %convolution_add_fusion.7, bf16[128,512]{1,0:T(8,128)(2,1)S(1)} %bitcast.80, f32[2048]{0:T(1024)S(1)} %get-tuple-element.405, f32[2048]{0:T(1024)S(1)} %get-tuple-element.406), kind=kOutput, calls=%fused_computation.16.clone.1 | convolution fusion | flops 288620544 | bytes 2244608 | tf_op jit(solution)/shard_map/while/body/eval_jaxpr/dot_general | solution.py:64
  429.2 18.4 %convolution_add_fusion.6 = f32[128,2048]{1,0:T(8,128)S(1)} fusion(bf16[128,512]{1,0:T(8,128)(2,1)S(1)} %bitcast.83, f32[2048]{0:T(1024)S(1)} %get-tuple-element.405, f32[2048]{0:T(1024)S(1)} %get-tuple-element.406, f32[128,2048]{1,0:T(8,128)S(1)} %get-tuple-element.419, pred[]{:T(512)S(6)} %compare.58), kind=kOutput, calls=%fused_computation.19.clone.1 | convolution fusion | flops 288882688 | bytes 2244609 | tf_op jit(solution)/shard_map/while/body/eval_jaxpr/dot_general | solution.py:58
  447.6 18.4 %convolution_subtract_fusion.2 = f32[128,2048]{1,0:T(8,128)S(1)} fusion(f32[128,2048]{1,0:T(8,128)S(1)} %convolution_add_fusion.6, bf16[128,512]{1,0:T(8,128)(2,1)S(1)} %bitcast.81, f32[2048]{0:T(1024)S(1)} %get-tuple-element.405, f32[2048]{0:T(1024)S(1)} %get-tuple-element.406), kind=kOutput, calls=%fused_computation.18.clone.1 | convolution fusion | flops 288620544 | bytes 2244608 | tf_op jit(solution)/shard_map/while/body/eval_jaxpr/dot_general | solution.py:59
  468.6 18.4 %convolution_add_fusion.7 = f32[128,2048]{1,0:T(8,128)S(1)} fusion(bf16[128,512]{1,0:T(8,128)(2,1)S(1)} %bitcast.82, f32[2048]{0:T(1024)S(1)} %get-tuple-element.405, f32[2048]{0:T(1024)S(1)} %get-tuple-element.406, f32[128,2048]{1,0:T(8,128)S(1)} %get-tuple-element.420, pred[]{:T(512)S(6)} %compare.58), kind=kOutput, calls=%fused_computation.17.clone.1 | convolution fusion | flops 288882688 | bytes 2244609 | tf_op jit(solution)/shard_map/while/body/eval_jaxpr/dot_general | solution.py:63
  486.9 18.4 %convolution_add_fusion.8 = f32[128,2048]{1,0:T(8,128)S(1)} fusion(f32[128,2048]{1,0:T(8,128)S(1)} %convolution_add_fusion.7, bf16[128,512]{1,0:T(8,128)(2,1)S(1)} %bitcast.80, f32[2048]{0:T(1024)S(1)} %get-tuple-element.405, f32[2048]{0:T(1024)S(1)} %get-tuple-element.406), kind=kOutput, calls=%fused_computation.16.clone.1 | convolution fusion | flops 288620544 | bytes 2244608 | tf_op jit(solution)/shard_map/while/body/eval_jaxpr/dot_general | solution.py:64
  505.3 18.4 %convolution_add_fusion.6 = f32[128,2048]{1,0:T(8,128)S(1)} fusion(bf16[128,512]{1,0:T(8,128)(2,1)S(1)} %bitcast.83, f32[2048]{0:T(1024)S(1)} %get-tuple-element.405, f32[2048]{0:T(1024)S(1)} %get-tuple-element.406, f32[128,2048]{1,0:T(8,128)S(1)} %get-tuple-element.419, pred[]{:T(512)S(6)} %compare.58), kind=kOutput, calls=%fused_computation.19.clone.1 | convolution fusion | flops 288882688 | bytes 2244609 | tf_op jit(solution)/shard_map/while/body/eval_jaxpr/dot_general | solution.py:58
  523.7 18.4 %convolution_subtract_fusion.2 = f32[128,2048]{1,0:T(8,128)S(1)} fusion(f32[128,2048]{1,0:T(8,128)S(1)} %convolution_add_fusion.6, bf16[128,512]{1,0:T(8,128)(2,1)S(1)} %bitcast.81, f32[2048]{0:T(1024)S(1)} %get-tuple-element.405, f32[2048]{0:T(1024)S(1)} %get-tuple-element.406), kind=kOutput, calls=%fused_computation.18.clone.1 | convolution fusion | flops 288620544 | bytes 2244608 | tf_op jit(solution)/shard_map/while/body/eval_jaxpr/dot_general | solution.py:59
  544.6 18.4 %convolution_add_fusion.7 = f32[128,2048]{1,0:T(8,128)S(1)} fusion(bf16[128,512]{1,0:T(8,128)(2,1)S(1)} %bitcast.82, f32[2048]{0:T(1024)S(1)} %get-tuple-element.405, f32[2048]{0:T(1024)S(1)} %get-tuple-element.406, f32[128,2048]{1,0:T(8,128)S(1)} %get-tuple-element.420, pred[]{:T(512)S(6)} %compare.58), kind=kOutput, calls=%fused_computation.17.clone.1 | convolution fusion | flops 288882688 | bytes 2244609 | tf_op jit(solution)/shard_map/while/body/eval_jaxpr/dot_general | solution.py:63
  563.0 18.4 %convolution_add_fusion.8 = f32[128,2048]{1,0:T(8,128)S(1)} fusion(f32[128,2048]{1,0:T(8,128)S(1)} %convolution_add_fusion.7, bf16[128,512]{1,0:T(8,128)(2,1)S(1)} %bitcast.80, f32[2048]{0:T(1024)S(1)} %get-tuple-element.405, f32[2048]{0:T(1024)S(1)} %get-tuple-element.406), kind=kOutput, calls=%fused_computation.16.clone.1 | convolution fusion | flops 288620544 | bytes 2244608 | tf_op jit(solution)/shard_map/while/body/eval_jaxpr/dot_general | solution.py:64
  581.4 18.4 %convolution_add_fusion.6 = f32[128,2048]{1,0:T(8,128)S(1)} fusion(bf16[128,512]{1,0:T(8,128)(2,1)S(1)} %bitcast.83, f32[2048]{0:T(1024)S(1)} %get-tuple-element.405, f32[2048]{0:T(1024)S(1)} %get-tuple-element.406, f32[128,2048]{1,0:T(8,128)S(1)} %get-tuple-element.419, pred[]{:T(512)S(6)} %compare.58), kind=kOutput, calls=%fused_computation.19.clone.1 | convolution fusion | flops 288882688 | bytes 2244609 | tf_op jit(solution)/shard_map/while/body/eval_jaxpr/dot_general | solution.py:58
  599.7 18.4 %convolution_subtract_fusion.2 = f32[128,2048]{1,0:T(8,128)S(1)} fusion(f32[128,2048]{1,0:T(8,128)S(1)} %convolution_add_fusion.6, bf16[128,512]{1,0:T(8,128)(2,1)S(1)} %bitcast.81, f32[2048]{0:T(1024)S(1)} %get-tuple-element.405, f32[2048]{0:T(1024)S(1)} %get-tuple-element.406), kind=kOutput, calls=%fused_computation.18.clone.1 | convolution fusion | flops 288620544 | bytes 2244608 | tf_op jit(solution)/shard_map/while/body/eval_jaxpr/dot_general | solution.py:59
  620.7 18.4 %convolution_add_fusion.7 = f32[128,2048]{1,0:T(8,128)S(1)} fusion(bf16[128,512]{1,0:T(8,128)(2,1)S(1)} %bitcast.82, f32[2048]{0:T(1024)S(1)} %get-tuple-element.405, f32[2048]{0:T(1024)S(1)} %get-tuple-element.406, f32[128,2048]{1,0:T(8,128)S(1)} %get-tuple-element.420, pred[]{:T(512)S(6)} %compare.58), kind=kOutput, calls=%fused_computation.17.clone.1 | convolution fusion | flops 288882688 | bytes 2244609 | tf_op jit(solution)/shard_map/while/body/eval_jaxpr/dot_general | solution.py:63
  639.1 18.4 %convolution_add_fusion.8 = f32[128,2048]{1,0:T(8,128)S(1)} fusion(f32[128,2048]{1,0:T(8,128)S(1)} %convolution_add_fusion.7, bf16[128,512]{1,0:T(8,128)(2,1)S(1)} %bitcast.80, f32[2048]{0:T(1024)S(1)} %get-tuple-element.405, f32[2048]{0:T(1024)S(1)} %get-tuple-element.406), kind=kOutput, calls=%fused_computation.16.clone.1 | convolution fusion | flops 288620544 | bytes 2244608 | tf_op jit(solution)/shard_map/while/body/eval_jaxpr/dot_general | solution.py:64
  657.4 18.4 %convolution_add_fusion.6 = f32[128,2048]{1,0:T(8,128)S(1)} fusion(bf16[128,512]{1,0:T(8,128)(2,1)S(1)} %bitcast.83, f32[2048]{0:T(1024)S(1)} %get-tuple-element.405, f32[2048]{0:T(1024)S(1)} %get-tuple-element.406, f32[128,2048]{1,0:T(8,128)S(1)} %get-tuple-element.419, pred[]{:T(512)S(6)} %compare.58), kind=kOutput, calls=%fused_computation.19.clone.1 | convolution fusion | flops 288882688 | bytes 2244609 | tf_op jit(solution)/shard_map/while/body/eval_jaxpr/dot_general | solution.py:58
  675.8 18.4 %convolution_subtract_fusion.2 = f32[128,2048]{1,0:T(8,128)S(1)} fusion(f32[128,2048]{1,0:T(8,128)S(1)} %convolution_add_fusion.6, bf16[128,512]{1,0:T(8,128)(2,1)S(1)} %bitcast.81, f32[2048]{0:T(1024)S(1)} %get-tuple-element.405, f32[2048]{0:T(1024)S(1)} %get-tuple-element.406), kind=kOutput, calls=%fused_computation.18.clone.1 | convolution fusion | flops 288620544 | bytes 2244608 | tf_op jit(solution)/shard_map/while/body/eval_jaxpr/dot_general | solution.py:59
  696.8 18.4 %convolution_add_fusion.7 = f32[128,2048]{1,0:T(8,128)S(1)} fusion(bf16[128,512]{1,0:T(8,128)(2,1)S(1)} %bitcast.82, f32[2048]{0:T(1024)S(1)} %get-tuple-element.405, f32[2048]{0:T(1024)S(1)} %get-tuple-element.406, f32[128,2048]{1,0:T(8,128)S(1)} %get-tuple-element.420, pred[]{:T(512)S(6)} %compare.58), kind=kOutput, calls=%fused_computation.17.clone.1 | convolution fusion | flops 288882688 | bytes 2244609 | tf_op jit(solution)/shard_map/while/body/eval_jaxpr/dot_general | solution.py:63
  715.1 18.4 %convolution_add_fusion.8 = f32[128,2048]{1,0:T(8,128)S(1)} fusion(f32[128,2048]{1,0:T(8,128)S(1)} %convolution_add_fusion.7, bf16[128,512]{1,0:T(8,128)(2,1)S(1)} %bitcast.80, f32[2048]{0:T(1024)S(1)} %get-tuple-element.405, f32[2048]{0:T(1024)S(1)} %get-tuple-element.406), kind=kOutput, calls=%fused_computation.16.clone.1 | convolution fusion | flops 288620544 | bytes 2244608 | tf_op jit(solution)/shard_map/while/body/eval_jaxpr/dot_general | solution.py:64
  733.5 18.4 %convolution_add_fusion.6 = f32[128,2048]{1,0:T(8,128)S(1)} fusion(bf16[128,512]{1,0:T(8,128)(2,1)S(1)} %bitcast.83, f32[2048]{0:T(1024)S(1)} %get-tuple-element.405, f32[2048]{0:T(1024)S(1)} %get-tuple-element.406, f32[128,2048]{1,0:T(8,128)S(1)} %get-tuple-element.419, pred[]{:T(512)S(6)} %compare.58), kind=kOutput, calls=%fused_computation.19.clone.1 | convolution fusion | flops 288882688 | bytes 2244609 | tf_op jit(solution)/shard_map/while/body/eval_jaxpr/dot_general | solution.py:58
  751.9 18.4 %convolution_subtract_fusion.2 = f32[128,2048]{1,0:T(8,128)S(1)} fusion(f32[128,2048]{1,0:T(8,128)S(1)} %convolution_add_fusion.6, bf16[128,512]{1,0:T(8,128)(2,1)S(1)} %bitcast.81, f32[2048]{0:T(1024)S(1)} %get-tuple-element.405, f32[2048]{0:T(1024)S(1)} %get-tuple-element.406), kind=kOutput, calls=%fused_computation.18.clone.1 | convolution fusion | flops 288620544 | bytes 2244608 | tf_op jit(solution)/shard_map/while/body/eval_jaxpr/dot_general | solution.py:59
  772.9 18.4 %convolution_add_fusion.7 = f32[128,2048]{1,0:T(8,128)S(1)} fusion(bf16[128,512]{1,0:T(8,128)(2,1)S(1)} %bitcast.82, f32[2048]{0:T(1024)S(1)} %get-tuple-element.405, f32[2048]{0:T(1024)S(1)} %get-tuple-element.406, f32[128,2048]{1,0:T(8,128)S(1)} %get-tuple-element.420, pred[]{:T(512)S(6)} %compare.58), kind=kOutput, calls=%fused_computation.17.clone.1 | convolution fusion | flops 288882688 | bytes 2244609 | tf_op jit(solution)/shard_map/while/body/eval_jaxpr/dot_general | solution.py:63
  791.2 18.4 %convolution_add_fusion.8 = f32[128,2048]{1,0:T(8,128)S(1)} fusion(f32[128,2048]{1,0:T(8,128)S(1)} %convolution_add_fusion.7, bf16[128,512]{1,0:T(8,128)(2,1)S(1)} %bitcast.80, f32[2048]{0:T(1024)S(1)} %get-tuple-element.405, f32[2048]{0:T(1024)S(1)} %get-tuple-element.406), kind=kOutput, calls=%fused_computation.16.clone.1 | convolution fusion | flops 288620544 | bytes 2244608 | tf_op jit(solution)/shard_map/while/body/eval_jaxpr/dot_general | solution.py:64
  809.6 18.4 %convolution_add_fusion.6 = f32[128,2048]{1,0:T(8,128)S(1)} fusion(bf16[128,512]{1,0:T(8,128)(2,1)S(1)} %bitcast.83, f32[2048]{0:T(1024)S(1)} %get-tuple-element.405, f32[2048]{0:T(1024)S(1)} %get-tuple-element.406, f32[128,2048]{1,0:T(8,128)S(1)} %get-tuple-element.419, pred[]{:T(512)S(6)} %compare.58), kind=kOutput, calls=%fused_computation.19.clone.1 | convolution fusion | flops 288882688 | bytes 2244609 | tf_op jit(solution)/shard_map/while/body/eval_jaxpr/dot_general | solution.py:58
  828.0 18.4 %convolution_subtract_fusion.2 = f32[128,2048]{1,0:T(8,128)S(1)} fusion(f32[128,2048]{1,0:T(8,128)S(1)} %convolution_add_fusion.6, bf16[128,512]{1,0:T(8,128)(2,1)S(1)} %bitcast.81, f32[2048]{0:T(1024)S(1)} %get-tuple-element.405, f32[2048]{0:T(1024)S(1)} %get-tuple-element.406), kind=kOutput, calls=%fused_computation.18.clone.1 | convolution fusion | flops 288620544 | bytes 2244608 | tf_op jit(solution)/shard_map/while/body/eval_jaxpr/dot_general | solution.py:59
  848.9 18.4 %convolution_add_fusion.7 = f32[128,2048]{1,0:T(8,128)S(1)} fusion(bf16[128,512]{1,0:T(8,128)(2,1)S(1)} %bitcast.82, f32[2048]{0:T(1024)S(1)} %get-tuple-element.405, f32[2048]{0:T(1024)S(1)} %get-tuple-element.406, f32[128,2048]{1,0:T(8,128)S(1)} %get-tuple-element.420, pred[]{:T(512)S(6)} %compare.58), kind=kOutput, calls=%fused_computation.17.clone.1 | convolution fusion | flops 288882688 | bytes 2244609 | tf_op jit(solution)/shard_map/while/body/eval_jaxpr/dot_general | solution.py:63
  867.3 18.4 %convolution_add_fusion.8 = f32[128,2048]{1,0:T(8,128)S(1)} fusion(f32[128,2048]{1,0:T(8,128)S(1)} %convolution_add_fusion.7, bf16[128,512]{1,0:T(8,128)(2,1)S(1)} %bitcast.80, f32[2048]{0:T(1024)S(1)} %get-tuple-element.405, f32[2048]{0:T(1024)S(1)} %get-tuple-element.406), kind=kOutput, calls=%fused_computation.16.clone.1 | convolution fusion | flops 288620544 | bytes 2244608 | tf_op jit(solution)/shard_map/while/body/eval_jaxpr/dot_general | solution.py:64
  885.7 18.4 %convolution_add_fusion.6 = f32[128,2048]{1,0:T(8,128)S(1)} fusion(bf16[128,512]{1,0:T(8,128)(2,1)S(1)} %bitcast.83, f32[2048]{0:T(1024)S(1)} %get-tuple-element.405, f32[2048]{0:T(1024)S(1)} %get-tuple-element.406, f32[128,2048]{1,0:T(8,128)S(1)} %get-tuple-element.419, pred[]{:T(512)S(6)} %compare.58), kind=kOutput, calls=%fused_computation.19.clone.1 | convolution fusion | flops 288882688 | bytes 2244609 | tf_op jit(solution)/shard_map/while/body/eval_jaxpr/dot_general | solution.py:58
  904.0 18.4 %convolution_subtract_fusion.2 = f32[128,2048]{1,0:T(8,128)S(1)} fusion(f32[128,2048]{1,0:T(8,128)S(1)} %convolution_add_fusion.6, bf16[128,512]{1,0:T(8,128)(2,1)S(1)} %bitcast.81, f32[2048]{0:T(1024)S(1)} %get-tuple-element.405, f32[2048]{0:T(1024)S(1)} %get-tuple-element.406), kind=kOutput, calls=%fused_computation.18.clone.1 | convolution fusion | flops 288620544 | bytes 2244608 | tf_op jit(solution)/shard_map/while/body/eval_jaxpr/dot_general | solution.py:59
  925.0 18.4 %convolution_add_fusion.7 = f32[128,2048]{1,0:T(8,128)S(1)} fusion(bf16[128,512]{1,0:T(8,128)(2,1)S(1)} %bitcast.82, f32[2048]{0:T(1024)S(1)} %get-tuple-element.405, f32[2048]{0:T(1024)S(1)} %get-tuple-element.406, f32[128,2048]{1,0:T(8,128)S(1)} %get-tuple-element.420, pred[]{:T(512)S(6)} %compare.58), kind=kOutput, calls=%fused_computation.17.clone.1 | convolution fusion | flops 288882688 | bytes 2244609 | tf_op jit(solution)/shard_map/while/body/eval_jaxpr/dot_general | solution.py:63
  943.4 18.4 %convolution_add_fusion.8 = f32[128,2048]{1,0:T(8,128)S(1)} fusion(f32[128,2048]{1,0:T(8,128)S(1)} %convolution_add_fusion.7, bf16[128,512]{1,0:T(8,128)(2,1)S(1)} %bitcast.80, f32[2048]{0:T(1024)S(1)} %get-tuple-element.405, f32[2048]{0:T(1024)S(1)} %get-tuple-element.406), kind=kOutput, calls=%fused_computation.16.clone.1 | convolution fusion | flops 288620544 | bytes 2244608 | tf_op jit(solution)/shard_map/while/body/eval_jaxpr/dot_general | solution.py:64
  961.7 18.4 %convolution_add_fusion.6 = f32[128,2048]{1,0:T(8,128)S(1)} fusion(bf16[128,512]{1,0:T(8,128)(2,1)S(1)} %bitcast.83, f32[2048]{0:T(1024)S(1)} %get-tuple-element.405, f32[2048]{0:T(1024)S(1)} %get-tuple-element.406, f32[128,2048]{1,0:T(8,128)S(1)} %get-tuple-element.419, pred[]{:T(512)S(6)} %compare.58), kind=kOutput, calls=%fused_computation.19.clone.1 | convolution fusion | flops 288882688 | bytes 2244609 | tf_op jit(solution)/shard_map/while/body/eval_jaxpr/dot_general | solution.py:58
  980.1 18.4 %convolution_subtract_fusion.2 = f32[128,2048]{1,0:T(8,128)S(1)} fusion(f32[128,2048]{1,0:T(8,128)S(1)} %convolution_add_fusion.6, bf16[128,512]{1,0:T(8,128)(2,1)S(1)} %bitcast.81, f32[2048]{0:T(1024)S(1)} %get-tuple-element.405, f32[2048]{0:T(1024)S(1)} %get-tuple-element.406), kind=kOutput, calls=%fused_computation.18.clone.1 | convolution fusion | flops 288620544 | bytes 2244608 | tf_op jit(solution)/shard_map/while/body/eval_jaxpr/dot_general | solution.py:59
  1001.1 18.4 %convolution_add_fusion.7 = f32[128,2048]{1,0:T(8,128)S(1)} fusion(bf16[128,512]{1,0:T(8,128)(2,1)S(1)} %bitcast.82, f32[2048]{0:T(1024)S(1)} %get-tuple-element.405, f32[2048]{0:T(1024)S(1)} %get-tuple-element.406, f32[128,2048]{1,0:T(8,128)S(1)} %get-tuple-element.420, pred[]{:T(512)S(6)} %compare.58), kind=kOutput, calls=%fused_computation.17.clone.1 | convolution fusion | flops 288882688 | bytes 2244609 | tf_op jit(solution)/shard_map/while/body/eval_jaxpr/dot_general | solution.py:63
  1019.4 18.4 %convolution_add_fusion.8 = f32[128,2048]{1,0:T(8,128)S(1)} fusion(f32[128,2048]{1,0:T(8,128)S(1)} %convolution_add_fusion.7, bf16[128,512]{1,0:T(8,128)(2,1)S(1)} %bitcast.80, f32[2048]{0:T(1024)S(1)} %get-tuple-element.405, f32[2048]{0:T(1024)S(1)} %get-tuple-element.406), kind=kOutput, calls=%fused_computation.16.clone.1 | convolution fusion | flops 288620544 | bytes 2244608 | tf_op jit(solution)/shard_map/while/body/eval_jaxpr/dot_general | solution.py:64
  1037.8 18.4 %convolution_add_fusion.6 = f32[128,2048]{1,0:T(8,128)S(1)} fusion(bf16[128,512]{1,0:T(8,128)(2,1)S(1)} %bitcast.83, f32[2048]{0:T(1024)S(1)} %get-tuple-element.405, f32[2048]{0:T(1024)S(1)} %get-tuple-element.406, f32[128,2048]{1,0:T(8,128)S(1)} %get-tuple-element.419, pred[]{:T(512)S(6)} %compare.58), kind=kOutput, calls=%fused_computation.19.clone.1 | convolution fusion | flops 288882688 | bytes 2244609 | tf_op jit(solution)/shard_map/while/body/eval_jaxpr/dot_general | solution.py:58
  1056.2 18.4 %convolution_subtract_fusion.2 = f32[128,2048]{1,0:T(8,128)S(1)} fusion(f32[128,2048]{1,0:T(8,128)S(1)} %convolution_add_fusion.6, bf16[128,512]{1,0:T(8,128)(2,1)S(1)} %bitcast.81, f32[2048]{0:T(1024)S(1)} %get-tuple-element.405, f32[2048]{0:T(1024)S(1)} %get-tuple-element.406), kind=kOutput, calls=%fused_computation.18.clone.1 | convolution fusion | flops 288620544 | bytes 2244608 | tf_op jit(solution)/shard_map/while/body/eval_jaxpr/dot_general | solution.py:59
  1077.2 18.4 %convolution_add_fusion.7 = f32[128,2048]{1,0:T(8,128)S(1)} fusion(bf16[128,512]{1,0:T(8,128)(2,1)S(1)} %bitcast.82, f32[2048]{0:T(1024)S(1)} %get-tuple-element.405, f32[2048]{0:T(1024)S(1)} %get-tuple-element.406, f32[128,2048]{1,0:T(8,128)S(1)} %get-tuple-element.420, pred[]{:T(512)S(6)} %compare.58), kind=kOutput, calls=%fused_computation.17.clone.1 | convolution fusion | flops 288882688 | bytes 2244609 | tf_op jit(solution)/shard_map/while/body/eval_jaxpr/dot_general | solution.py:63
  1113.9 18.4 %convolution_add_fusion.6 = f32[128,2048]{1,0:T(8,128)S(1)} fusion(bf16[128,512]{1,0:T(8,128)(2,1)S(1)} %bitcast.83, f32[2048]{0:T(1024)S(1)} %get-tuple-element.405, f32[2048]{0:T(1024)S(1)} %get-tuple-element.406, f32[128,2048]{1,0:T(8,128)S(1)} %get-tuple-element.419, pred[]{:T(512)S(6)} %compare.58), kind=kOutput, calls=%fused_computation.19.clone.1 | convolution fusion | flops 288882688 | bytes 2244609 | tf_op jit(solution)/shard_map/while/body/eval_jaxpr/dot_general | solution.py:58
  1132.3 18.4 %convolution_subtract_fusion.2 = f32[128,2048]{1,0:T(8,128)S(1)} fusion(f32[128,2048]{1,0:T(8,128)S(1)} %convolution_add_fusion.6, bf16[128,512]{1,0:T(8,128)(2,1)S(1)} %bitcast.81, f32[2048]{0:T(1024)S(1)} %get-tuple-element.405, f32[2048]{0:T(1024)S(1)} %get-tuple-element.406), kind=kOutput, calls=%fused_computation.18.clone.1 | convolution fusion | flops 288620544 | bytes 2244608 | tf_op jit(solution)/shard_map/while/body/eval_jaxpr/dot_general | solution.py:59
  1153.2 18.4 %convolution_add_fusion.7 = f32[128,2048]{1,0:T(8,128)S(1)} fusion(bf16[128,512]{1,0:T(8,128)(2,1)S(1)} %bitcast.82, f32[2048]{0:T(1024)S(1)} %get-tuple-element.405, f32[2048]{0:T(1024)S(1)} %get-tuple-element.406, f32[128,2048]{1,0:T(8,128)S(1)} %get-tuple-element.420, pred[]{:T(512)S(6)} %compare.58), kind=kOutput, calls=%fused_computation.17.clone.1 | convolution fusion | flops 288882688 | bytes 2244609 | tf_op jit(solution)/shard_map/while/body/eval_jaxpr/dot_general | solution.py:63
  1171.6 18.4 %convolution_add_fusion.8 = f32[128,2048]{1,0:T(8,128)S(1)} fusion(f32[128,2048]{1,0:T(8,128)S(1)} %convolution_add_fusion.7, bf16[128,512]{1,0:T(8,128)(2,1)S(1)} %bitcast.80, f32[2048]{0:T(1024)S(1)} %get-tuple-element.405, f32[2048]{0:T(1024)S(1)} %get-tuple-element.406), kind=kOutput, calls=%fused_computation.16.clone.1 | convolution fusion | flops 288620544 | bytes 2244608 | tf_op jit(solution)/shard_map/while/body/eval_jaxpr/dot_general | solution.py:64
  1190.0 18.4 %convolution_add_fusion.6 = f32[128,2048]{1,0:T(8,128)S(1)} fusion(bf16[128,512]{1,0:T(8,128)(2,1)S(1)} %bitcast.83, f32[2048]{0:T(1024)S(1)} %get-tuple-element.405, f32[2048]{0:T(1024)S(1)} %get-tuple-element.406, f32[128,2048]{1,0:T(8,128)S(1)} %get-tuple-element.419, pred[]{:T(512)S(6)} %compare.58), kind=kOutput, calls=%fused_computation.19.clone.1 | convolution fusion | flops 288882688 | bytes 2244609 | tf_op jit(solution)/shard_map/while/body/eval_jaxpr/dot_general | solution.py:58
  1208.3 18.4 %convolution_subtract_fusion.2 = f32[128,2048]{1,0:T(8,128)S(1)} fusion(f32[128,2048]{1,0:T(8,128)S(1)} %convolution_add_fusion.6, bf16[128,512]{1,0:T(8,128)(2,1)S(1)} %bitcast.81, f32[2048]{0:T(1024)S(1)} %get-tuple-element.405, f32[2048]{0:T(1024)S(1)} %get-tuple-element.406), kind=kOutput, calls=%fused_computation.18.clone.1 | convolution fusion | flops 288620544 | bytes 2244608 | tf_op jit(solution)/shard_map/while/body/eval_jaxpr/dot_general | solution.py:59
  1229.0 77.0 %reduce-scatter.2.cloned.1.call-done = f32[8,16,2,256]{3,1,2,0:T(8,128)} async-done(((f32[8,16,2,2048]{3,1,2,0:T(8,128)}), f32[8,16,2,256]{3,1,2,0:T(8,128)}) %reduce-scatter.2.cloned.1.call-update) | async-done | bytes 262160 | tf_op jit(solution)/shard_map/reduce_scatter | solution.py:143
  1307.0 38.5 %all-gather.2.cloned.1.call-done = f32[8,256,2,256]{3,1,2,0:T(8,128)} async-done(((f32[8,16,2,256]{3,1,2,0:T(8,128)}), f32[8,256,2,256]{3,1,2,0:T(8,128)}) %all-gather.2.cloned.1.call-update) | async-done | bytes 4194320 | tf_op jit(solution)/shard_map/all_gather | solution.py:146
  (183 shorter events, 398.4 us)
Async XLA Ops:
  6.5 1299.5 %reduce-scatter.2.cloned.1.call-start = ((), (), s32[]{:S(2)}) async-start(), calls=%async_computation.2 | async-start | bytes 2359296 | tf_op jit(solution)/shard_map/reduce_scatter | solution.py:143
  1227.0 79.9 %copy-start.2 = (s32[8,2]{0,1:T(2,128)S(1)}, s32[8,2]{0,1:T(2,128)}, u32[]{:S(2)}) copy-start(s32[8,2]{0,1:T(2,128)} %param.15) | copy-start | bytes 196
  1227.0 79.9 %copy-start.1 = (s32[256]{0:T(256)S(1)}, s32[256]{0:T(256)}, u32[]{:S(2)}) copy-start(s32[256]{0:T(256)} %param.13) | copy-start | bytes 3076
  1228.5 117.0 %all-gather.2.cloned.1.call-start = ((), (), s32[]{:S(2)}) async-start(), calls=%async_computation.3 | async-start | bytes 4456448 | tf_op jit(solution)/shard_map/all_gather | solution.py:146
  1345.5 4.5 copy-start
  1352.8 12.9 all-to-all-start
Sparse Core Ops, SparseCore 0:
  1228.6 77.3 reduce-scatter.1
  1307.8 37.6 all-gather.1
where the time goes:
time: 1660 us; the launch traced here: 1650 us
  matrix products  1460 us (88%)
  waiting for transfers between devices  122 us (7%)
  other arithmetic  32.2 us (2%)
    dot_general x16, matrix products, one_block(): jnp.dot(g_real, t_imag, preferred_element_type=f32)  294 us
    dot_general x16, matrix products, one_block(): jnp.dot(g_real, t_real, preferred_element_type=f32)  294 us
    dot_general x16, matrix products, one_block(): jnp.dot(g_imag, t_imag, preferred_element_type=f32)  294 us
    dot_general x16, matrix products, one_block(): jnp.dot(g_imag, t_real, preferred_element_type=f32)  294 us
    reduce_scatter x1, waiting for transfers between devices, local(): lax.psum_scatter(contrib, 'facet', scatter_dimension=3, tiled=True)  77 us
    dot_general x4, matrix products, finish(): jnp.dot(imag_in, t_sin, preferred_element_type=f32)  69.2 us
    dot_general x4, matrix products, finish(): jnp.dot(real_in, t_cos, preferred_element_type=f32)  69.2 us
    dot_general x4, matrix products, finish(): jnp.dot(real_in, t_sin, preferred_element_type=f32)  68.9 us
  transfers between devices with their start and end apart: 3, of which 3 were waited for; matrix products, arithmetic and copies ran while one was open for 0% of the time, Pallas kernels for 0%

commit v1 on v0

v1 whole, which is shorter than its diff:
```python
import math

import jax
import jax.numpy as jnp
from jax import lax
from jax.experimental import pallas as pl
from jax.experimental.pallas import tpu as pltpu
from jax.sharding import PartitionSpec as P

MESH = pl.DeviceIdType.MESH
F32 = jnp.float32
BF16 = jnp.bfloat16
NF = 8
NS = 16
ROWS = 256
XW = 512
NI = 256
SG = 2048


def cs(n):
    quad = (n + 8192) >> 14
    th = (n - (quad << 14)).astype(F32) * (2.0 * math.pi / 65536)
    t2 = th * th
    s = th * (1.0 + t2 * (-1.0 / 6 + t2 * (1.0 / 120 - t2 * (1.0 / 5040))))
    c = 1.0 + t2 * (-0.5 + t2 * (1.0 / 24 + t2 * (-1.0 / 720 + t2 * (1.0 / 40320))))
    odd = (quad & 1) == 1
    cos = jnp.where(odd, s, c)
    sin = jnp.where(odd, c, s)
    cos = jnp.where(((quad + 1) & 2) == 2, -cos, cos)
    sin = jnp.where((quad & 2) == 2, -sin, sin)
    return cos, sin


def iota(shape, dim):
    return lax.broadcasted_iota(jnp.int32, shape, dim)


def cmul(a, b):
    return a[0] * b[0] - a[1] * b[1], a[0] * b[1] + a[1] * b[0]


def cadd(a, b):
    return a[0] + b[0], a[1] + b[1]


def csub(a, b):
    return a[0] - b[0], a[1] - b[1]


def times_i(a):
    return -a[1], a[0]


def dft4(x0, x1, x2, x3):
    a, b = cadd(x0, x2), csub(x0, x2)
    c, d = cadd(x1, x3), times_i(csub(x1, x3))
    return cadd(a, c), cadd(b, d), csub(a, c), csub(b, d)


def dft8(t):
    even = dft4(t[0], t[2], t[4], t[6])
    odd = dft4(t[1], t[3], t[5], t[7])
    h = math.sqrt(0.5)
    o1 = ((odd[1][0] - odd[1][1]) * h, (odd[1][0] + odd[1][1]) * h)
    o2 = times_i(odd[2])
    o3 = ((-odd[3][0] - odd[3][1]) * h, (odd[3][0] - odd[3][1]) * h)
    odd = (odd[0], o1, o2, o3)
    return [cadd(e, o) for e, o in zip(even, odd)] + [csub(e, o) for e, o in zip(even, odd)]


def split(v):
    high = v.astype(BF16)
    return high, (v - high.astype(F32)).astype(BF16)


def kernel(
    d_ref, win_ref, pos_ref, fo_ref, so_ref, band_ref, ext_ref, out_ref,
    buf1, e_ref, send2, buf2, fb, send3, buf3, a_ref, w_ref, z_ref, send4, buf4, v_ref, tp_ref,
    s1, r1, s2, r2, s3, r3, s4, r4, loc,
):
    fi = lax.axis_index("facet")
    si = lax.axis_index("sub")
    m_own = si // 2
    jh = si % 2
    dest4 = 2 * fi + jh
    src4 = si // 2
    self4 = (fi == si // 2).astype(jnp.int32)

    barrier = pltpu.get_barrier_semaphore()

    def greet(f, s):
        pl.semaphore_signal(barrier, inc=1, device_id=(f, s), device_id_type=MESH)

    def greet_sub(k, c):
        greet(fi, (si + k) % NS)
        return c

    def greet_facet(k, c):
        greet((fi + k) % NF, si)
        return c

    def greet_last(m, c):
        @pl.when(jnp.logical_not(jnp.logical_and(src4 == fi, m == m_own)))
        def _():
            greet(src4, 2 * m + jh)

        return c

    lax.fori_loop(1, NS, greet_sub, 0)
    lax.fori_loop(1, NF, greet_facet, 0)
    lax.fori_loop(0, NF, greet_last, 0)
    pl.semaphore_wait(barrier, NS - 1 + NF - 1 + NF - self4)

    def copy1(k):
        to = (si + k) % NS
        return pltpu.make_async_remote_copy(
            src_ref=d_ref.at[:, :, pl.ds(pl.multiple_of(to * XW, XW), XW)],
            dst_ref=buf1.at[:, pl.ds(pl.multiple_of(si * 16, 16), 16), :],
            send_sem=s1.at[k], recv_sem=r1.at[k],
            device_id=(fi, to), device_id_type=MESH,
        )

    def go1(k, c):
        copy1(k).start()
        return c

    lax.fori_loop(1, NS, go1, 0)
    own1 = pltpu.make_async_copy(
        d_ref.at[:, :, pl.ds(pl.multiple_of(si * XW, XW), XW)],
        buf1.at[:, pl.ds(pl.multiple_of(si * 16, 16), 16), :],
        loc.at[0],
    )
    own1.start()

    band = band_ref[0]
    pos = pos_ref[...]

    def row_table(g, c):
        t = pos * (iota((8, ROWS), 0) + (8 * g + band))
        cos, sin = cs(t)
        for col, blk in ((0, (cos, -sin)), (1, (sin, cos))):
            high, low = split(jnp.concatenate(blk, axis=0))
            e_ref[0, pl.ds(pl.multiple_of(16 * g, 16), 16), pl.ds(col * ROWS, ROWS)] = high
            e_ref[1, pl.ds(pl.multiple_of(16 * g, 16), 16), pl.ds(col * ROWS, ROWS)] = low
        return c

    lax.fori_loop(0, 16, row_table, 0)

    lane = iota((1, 256), 1)
    off = jnp.zeros((1, 256), jnp.int32)
    for b in range(NF):
        off = jnp.where((lane >> 5) == b, fo_ref[b], off)

    def facet_table(g, c):
        row = iota((32, 256), 0)
        col = iota((32, 256), 1)
        cos, sin = cs(jnp.broadcast_to(off * (g * 8192), (32, 256)))
        rc, cc = (row >> 3) & 1, (col >> 3) & 1
        val = jnp.where(rc == cc, cos, jnp.where(rc == 0, sin, -sin))
        val = jnp.where(((row ^ col) & 0b10111) == 0, val, 0.0)
        fb[pl.ds(pl.multiple_of(32 * g, 32), 32), :] = val.astype(BF16)
        return c

    lax.fori_loop(0, NF, facet_table, 0)

    def first_freq(q):
        o = so_ref[q]
        return o + ((m_own - o) & 7)

    lane = iota((1, 128), 1)
    freq = jnp.zeros((1, 128), jnp.int32)
    for q in range(NF):
        freq = jnp.where(lane == q, first_freq(q), freq)

    def column_table(ac, c):
        step = 32
        a0 = ac * step
        base = cs((iota((step, NI), 0) + a0) * iota((step, NI), 1) * 8)
        ph = cs((iota((step, 128), 0) + a0) * freq)
        for q in range(NF):
            pq = (
                jnp.broadcast_to(ph[0][:, q : q + 1], (step, NI)),
                jnp.broadcast_to(ph[1][:, q : q + 1], (step, NI)),
            )
            cos, sin = cmul(base, pq)
            cos = cos.astype(BF16)
            sin = sin.astype(BF16)
            top = pl.ds(pl.multiple_of(a0, step), step)
            low = pl.ds(pl.multiple_of(a0 + XW, step), step)
            w_ref[q, top, pl.ds(0, NI)] = cos
            w_ref[q, top, pl.ds(NI, NI)] = -sin
            w_ref[q, low, pl.ds(0, NI)] = sin
            w_ref[q, low, pl.ds(NI, NI)] = cos
        return c

    lax.fori_loop(0, XW // 32, column_table, 0)

    fq = jnp.zeros((NF, NI), jnp.int32)
    for q in range(NF):
        fq = jnp.where(iota((NF, NI), 0) == q, first_freq(q), fq)
    fq = fq + 8 * iota((NF, NI), 1)
    z1 = cs(fq * 512)
    z2 = cs(fq * 1024)
    z_ref[0], z_ref[1] = z1[0], -z1[1]
    z_ref[2], z_ref[3] = z2[0], -z2[1]

    def sub_table(g, c):
        cos, sin = cs((iota((32, NI), 0) + 32 * g) * iota((32, NI), 1) * 256)
        at = pl.ds(pl.multiple_of(32 * g, 32), 32)
        for n, part in enumerate((cos, sin)):
            high, low = split(part)
            v_ref[0, at, pl.ds(n * NI, NI)] = high
            v_ref[1, at, pl.ds(n * NI, NI)] = low
        return c

    lax.fori_loop(0, 8, sub_table, 0)

    own1.wait()

    def wait1(k, c):
        pltpu.make_async_remote_copy(
            src_ref=d_ref.at[:, :, pl.ds(0, XW)],
            dst_ref=buf1.at[:, pl.ds(pl.multiple_of(((si - k + NS) % NS) * 16, 16), 16), :],
            send_sem=s1.at[k], recv_sem=r1.at[k],
            device_id=(fi, si), device_id_type=MESH,
        ).wait_recv()
        return c

    lax.fori_loop(1, NS, wait1, 0)

    data = buf1[...].reshape(2 * ROWS, XW)
    rows = jnp.dot(e_ref[0], data, preferred_element_type=F32) + jnp.dot(
        e_ref[1], data, preferred_element_type=F32
    )
    send2[...] = rows.astype(BF16).reshape(NF, 32, XW)

    def copy2(k):
        to = (fi + k) % NF
        return pltpu.make_async_remote_copy(
            src_ref=send2.at[to], dst_ref=buf2.at[fi],
            send_sem=s2.at[k], recv_sem=r2.at[k],
            device_id=(to, si), device_id_type=MESH,
        )

    def go2(k, c):
        copy2(k).start()
        return c

    lax.fori_loop(1, NF, go2, 0)
    own2 = pltpu.make_async_copy(send2.at[fi], buf2.at[fi], loc.at[1])
    own2.start()
    own2.wait()

    def wait2(k, c):
        pltpu.make_async_remote_copy(
            src_ref=send2.at[0], dst_ref=buf2.at[(fi - k + NF) % NF],
            send_sem=s2.at[k], recv_sem=r2.at[k],
            device_id=(fi, si), device_id_type=MESH,
        ).wait_recv()
        return c

    lax.fori_loop(1, NF, wait2, 0)

    win = win_ref[:, pl.ds(pl.multiple_of(si * XW, XW), XW)]
    summed = jnp.dot(fb[...], buf2[...].reshape(256, XW), preferred_element_type=F32)
    send3[...] = (summed * win).astype(BF16).reshape(NS, 16, XW)

    def copy3(k):
        to = (si + k) % NS
        return pltpu.make_async_remote_copy(
            src_ref=send3.at[to], dst_ref=buf3.at[si],
            send_sem=s3.at[k], recv_sem=r3.at[k],
            device_id=(fi, to), device_id_type=MESH,
        )

    def go3(k, c):
        copy3(k).start()
        return c

    lax.fori_loop(1, NS, go3, 0)
    own3 = pltpu.make_async_copy(send3.at[si], buf3.at[si], loc.at[2])
    own3.start()
    own3.wait()

    def wait3(k, c):
        pltpu.make_async_remote_copy(
            src_ref=send3.at[0], dst_ref=buf3.at[(si - k + NS) % NS],
            send_sem=s3.at[k], recv_sem=r3.at[k],
            device_id=(fi, si), device_id_type=MESH,
        ).wait_recv()
        return c

    lax.fori_loop(1, NS, wait3, 0)

    for t in range(8):
        one = buf3[2 * t].astype(F32)
        two = buf3[2 * t + 1].astype(F32)
        for c in range(2):
            part = jnp.concatenate([one[8 * c : 8 * c + 8], two[8 * c : 8 * c + 8]], axis=0)
            a_ref[pl.ds(16 * t, 16), pl.ds(c * XW, XW)] = part.astype(BF16)

    def copy4(q):
        return pltpu.make_async_remote_copy(
            src_ref=send4.at[q], dst_ref=buf4.at[m_own],
            send_sem=s4.at[q], recv_sem=r4.at[m_own],
            device_id=(q, dest4), device_id_type=MESH,
        )

    def own4():
        return pltpu.make_async_copy(send4.at[fi], buf4.at[m_own], loc.at[3])

    def columns(q, c):
        y = jnp.dot(a_ref[...], w_ref[q], preferred_element_type=F32)

        def part(e):
            return y[8 * e : 8 * e + 8, :NI], y[8 * e : 8 * e + 8, NI:]

        def row(n):
            return jnp.broadcast_to(z_ref[n, pl.ds(q, 1), :], (8, NI))

        zz = (row(2), row(3))
        even, odd = part(14), part(15)
        for e in range(12, -1, -2):
            even = cadd(cmul(even, zz), part(e))
            odd = cadd(cmul(odd, zz), part(e + 1))
        total = cadd(even, cmul(odd, (row(0), row(1))))
        k = ((m_own - so_ref[q]) & 7) + 8 * iota((8, NI), 1)
        keep = jnp.logical_and(k >= ext_ref[q, 0], k < SG - ext_ref[q, 1])
        both = jnp.concatenate(
            [jnp.where(keep, total[0], 0.0), jnp.where(keep, total[1], 0.0)], axis=0
        )
        send4[q] = both.astype(BF16)
        mine = jnp.logical_and(q == fi, dest4 == si)

        @pl.when(mine)
        def _():
            own4().start()

        @pl.when(jnp.logical_not(mine))
        def _():
            copy4(q).start()

        return c

    lax.fori_loop(0, NF, columns, 0)

    def wait4(m, c):
        mine = jnp.logical_and(src4 == fi, m == m_own)

        @pl.when(mine)
        def _():
            own4().wait()

        @pl.when(jnp.logical_not(mine))
        def _():
            pltpu.make_async_remote_copy(
                src_ref=send4.at[0], dst_ref=buf4.at[m],
                send_sem=s4.at[0], recv_sem=r4.at[m],
                device_id=(fi, si), device_id_type=MESH,
            ).wait_recv()

        return c

    tw = cs(iota((NF, NI), 0) * iota((NF, NI), 1) * 32)
    lax.fori_loop(0, NF, wait4, 0)

    got = buf4[...].reshape(128, NI)
    spec = jnp.dot(got, v_ref[0], preferred_element_type=F32) + jnp.dot(
        got, v_ref[1], preferred_element_type=F32
    )
    for m in range(NF):
        re, im = spec[16 * m : 16 * m + 8], spec[16 * m + 8 : 16 * m + 16]
        tp_ref[m, 0] = re[:, :NI] - im[:, NI:]
        tp_ref[m, 1] = re[:, NI:] + im[:, :NI]
    own = so_ref[fi]
    terms = []
    for kap in range(NF):
        got = tp_ref[(own + kap) & 7]
        step = (
            jnp.broadcast_to(tw[0][kap : kap + 1], (8, NI)),
            jnp.broadcast_to(tw[1][kap : kap + 1], (8, NI)),
        )
        terms.append(cmul((got[0], got[1]), step))
    scale = 1.0 / (4096.0 * math.sqrt(SG))
    for n, val in enumerate(dft8(terms)):
        out_ref[0, :, pl.ds(n * NI, NI)] = val[0] * scale
        out_ref[1, :, pl.ds(n * NI, NI)] = val[1] * scale

    def done1(k, c):
        copy1(k).wait_send()
        copy3(k).wait_send()
        return c

    def done2(k, c):
        copy2(k).wait_send()
        return c

    def done4(q, c):
        @pl.when(jnp.logical_not(jnp.logical_and(q == fi, dest4 == si)))
        def _():
            copy4(q).wait_send()

        return c

    lax.fori_loop(1, NS, done1, 0)
    lax.fori_loop(1, NF, done2, 0)
    lax.fori_loop(0, NF, done4, 0)


def local(slab, window, facet_offsets, subgrid_offsets, row_positions, band_offset, extents):
    vmem = pl.BlockSpec(memory_space=pltpu.VMEM)
    smem = pl.BlockSpec(memory_space=pltpu.SMEM)
    dma = pltpu.SemaphoreType.DMA
    out = pl.pallas_call(
        kernel,
        out_shape=jax.ShapeDtypeStruct((2, 8, SG), F32),
        in_specs=[pl.BlockSpec(memory_space=pl.ANY), vmem, vmem, smem, smem, smem, smem],
        out_specs=vmem,
        scratch_shapes=[
            pltpu.VMEM((2, ROWS, XW), BF16),
            pltpu.VMEM((2, ROWS, 2 * ROWS), BF16),
            pltpu.VMEM((NF, 32, XW), BF16),
            pltpu.VMEM((NF, 32, XW), BF16),
            pltpu.VMEM((256, 256), BF16),
            pltpu.VMEM((NS, 16, XW), BF16),
            pltpu.VMEM((NS, 16, XW), BF16),
            pltpu.VMEM((128, 2 * XW), BF16),
            pltpu.VMEM((NF, 2 * XW, 2 * NI), BF16),
            pltpu.VMEM((4, NF, NI), F32),
            pltpu.VMEM((NF, 16, NI), BF16),
            pltpu.VMEM((NF, 16, NI), BF16),
            pltpu.VMEM((2, NI, 2 * NI), BF16),
            pltpu.VMEM((NF, 2, 8, NI), F32),
            dma((NS,)), dma((NS,)), dma((NF,)), dma((NF,)),
            dma((NS,)), dma((NS,)), dma((NF,)), dma((NF,)), dma((4,)),
        ],
        compiler_params=pltpu.CompilerParams(
            collective_id=0, has_side_effects=True, vmem_limit_bytes=40 << 20
        ),
    )(
        slab.transpose(1, 0, 2), window.reshape(1, -1), row_positions.reshape(1, -1),
        facet_offsets, subgrid_offsets, band_offset, extents,
    )
    return out.transpose(1, 0, 2)[:, None]


def solution(mesh):
    return jax.shard_map(
        local,
        mesh=mesh,
        in_specs=(P("sub", None, "facet"), P(), P(), P(), P(), P(), P()),
        out_specs=P("sub", "facet", None, None),
        check_vma=False,
    )
```

time: 1660 us -> 41.5 us (0.03)
  the two profiles are of different devices: /device:TPU:1 before, /device:TPU:26 now
where the time goes in v1:
time: 41.5 us; the launch traced here: 41.3 us
  Pallas kernels  37.1 us (89%)
  local copies, waits for them, and re-layouts  3.51 us (8%)
  between operations  0.7 us (2%)
    pallas_call x1, Pallas kernels, local(): pl.pallas_call(kernel, out_shape=jax.ShapeDtypeStruct((2, 8, SG), F32), i...  37.1 us
    unnamed x12, local copies, waits for them, and re-layouts  2.75 us

profile of v1, /device:TPU:26, one launch (start us, length us, event | category | flops | bytes accessed | tf_op | source)
XLA Modules:
  0.0 41.3 jit_solution(15851222930627340348)
XLA Ops:
  0.7 0.0 copy-start.4
  0.7 0.7 %copy-done.4 = s32[8,2]{0,1:T(2,128)S(1)} copy-done((s32[8,2]{0,1:T(2,128)S(1)}, s32[8,2]{0,1:T(2,128)}, u32[]{:S(2)}) %copy-start.4) | copy-done | bytes 88
  1.3 0.1 copy.9.ext_ref
  1.4 0.0 copy-start
  1.4 0.0 copy-start.3
  1.4 1.3 %copy.12 = bf16[16,2,8192]{2,0,1:T(8,128)(2,1)S(1)} copy(bf16[16,2,8192]{2,1,0:T(2,128)(2,1)} %param.7) | data formatting | bytes 1048576 | tf_op args[0]
  2.8 0.0 copy-start.1
  2.8 0.0 copy-start.2
  2.8 0.0 copy-done
  2.8 0.0 copy-done.3
  2.8 0.6 %copy-done.1 = s32[256]{0:T(256)S(1)} copy-done((s32[256]{0:T(256)S(1)}, s32[256]{0:T(256)}, u32[]{:S(2)}) %copy-start.1) | copy-done | bytes 1048
  3.4 0.0 copy-done.2
  3.4 37.1 %shard_map.73 = f32[2,8,2048]{2,1,0:T(8,128)S(1)} custom-call(bf16[2,16,8192]{2,1,0:T(8,128)(2,1)S(1)} %bitcast.8, f32[1,8192]{1,0:T(1,128)S(1)} %bitcast.10, s32[1,256]{1,0:T(1,128)S(1)} %bitcast.11, s32[8]{0:T(128)S(1)} %copy-done.2, s32[8]{0:T(128)S(1)} %copy-done.3, s32[1]{0:T(128)S(6)} %copy.13.band_ref, s32[8,2]{1,0:T(8,128)S(1)} %copy.9.ext_ref), custom_call_target="tpu_custom_call" | custom-call | tf_op jit(solution)/shard_map/pallas_call | solution.py:415
  40.6 0.8 %copy.10 = f32[8,1,2,2048]{3,2,1,0:T(2,128)} copy(f32[8,1,2,2048]{3,0,2,1:T(8,128)S(1)} %bitcast.9) | data formatting | bytes 262144 | tf_op jit(solution)/shard_map/broadcast_in_dim | solution.py:445
Async XLA Ops:
  0.7 0.7 %copy-start.4 = (s32[8,2]{0,1:T(2,128)S(1)}, s32[8,2]{0,1:T(2,128)}, u32[]{:S(2)}) copy-start(s32[8,2]{0,1:T(2,128)} %param.13) | copy-start | bytes 196
  1.4 1.4 %copy-start = (f32[8192]{0:T(1024)S(1)}, f32[8192]{0:T(1024)}, u32[]{:S(2)}) copy-start(f32[8192]{0:T(1024)} %param.8) | copy-start | bytes 98308
  1.4 1.4 %copy-start.3 = (s32[8]{0:T(128)S(1)}, s32[8]{0:T(128)}, u32[]{:S(2)}) copy-start(s32[8]{0:T(128)} %so_ref.1) | copy-start | bytes 100
  2.8 0.7 %copy-start.1 = (s32[256]{0:T(256)S(1)}, s32[256]{0:T(256)}, u32[]{:S(2)}) copy-start(s32[256]{0:T(256)} %param.11) | copy-start | bytes 3076
  2.8 0.7 %copy-start.2 = (s32[8]{0:T(128)S(1)}, s32[8]{0:T(128)}, u32[]{:S(2)}) copy-start(s32[8]{0:T(128)} %fo_ref.1) | copy-start | bytes 100

commit v2 on v1

v2 whole, which is shorter than its diff:
```python
import math

import jax
import jax.numpy as jnp
from jax import lax
from jax.experimental import pallas as pl
from jax.experimental.pallas import tpu as pltpu
from jax.sharding import PartitionSpec as P

MESH = pl.DeviceIdType.MESH
F32 = jnp.float32
BF16 = jnp.bfloat16
NF = 8
NS = 16
ROWS = 256
XW = 512
NI = 256
SG = 2048
C = 4
CW = XW // C
ORDER = tuple((step, ch) for step in "rfg" for ch in range(C))


def cs(n):
    quad = (n + 8192) >> 14
    th = (n - (quad << 14)).astype(F32) * (2.0 * math.pi / 65536)
    t2 = th * th
    s = th * (1.0 + t2 * (-1.0 / 6 + t2 * (1.0 / 120 - t2 * (1.0 / 5040))))
    c = 1.0 + t2 * (-0.5 + t2 * (1.0 / 24 + t2 * (-1.0 / 720 + t2 * (1.0 / 40320))))
    odd = (quad & 1) == 1
    cos = jnp.where(odd, s, c)
    sin = jnp.where(odd, c, s)
    cos = jnp.where(((quad + 1) & 2) == 2, -cos, cos)
    sin = jnp.where((quad & 2) == 2, -sin, sin)
    return cos, sin


def iota(shape, dim):
    return lax.broadcasted_iota(jnp.int32, shape, dim)


def cmul(a, b):
    return a[0] * b[0] - a[1] * b[1], a[0] * b[1] + a[1] * b[0]


def cadd(a, b):
    return a[0] + b[0], a[1] + b[1]


def csub(a, b):
    return a[0] - b[0], a[1] - b[1]


def times_i(a):
    return -a[1], a[0]


def dft4(x0, x1, x2, x3):
    a, b = cadd(x0, x2), csub(x0, x2)
    c, d = cadd(x1, x3), times_i(csub(x1, x3))
    return cadd(a, c), cadd(b, d), csub(a, c), csub(b, d)


def dft8(t):
    even = dft4(t[0], t[2], t[4], t[6])
    odd = dft4(t[1], t[3], t[5], t[7])
    h = math.sqrt(0.5)
    o1 = ((odd[1][0] - odd[1][1]) * h, (odd[1][0] + odd[1][1]) * h)
    o2 = times_i(odd[2])
    o3 = ((-odd[3][0] - odd[3][1]) * h, (odd[3][0] - odd[3][1]) * h)
    odd = (odd[0], o1, o2, o3)
    return [cadd(e, o) for e, o in zip(even, odd)] + [csub(e, o) for e, o in zip(even, odd)]


def split(v):
    high = v.astype(BF16)
    return high, (v - high.astype(F32)).astype(BF16)


def kernel(
    d_ref, win_hbm, pos_hbm, fo_hbm, so_hbm, band_hbm, ext_hbm, out_ref,
    win_ref, pos_ref, fo_ref, so_ref, band_ref, ext_ref,
    buf1, e_ref, send2, buf2, fb, send3, buf3, a_ref, w_ref, z_ref, send4, buf4, v_ref, tp_ref,
    sends, r1, r2, r3, r4, loc, small,
):
    fi = lax.axis_index("facet")
    si = lax.axis_index("sub")
    m_own = si >> 1
    jh = si & 1
    dest4 = 2 * fi + jh
    src4 = si >> 1
    is_own4 = fi == src4

    smalls = [
        pltpu.make_async_copy(src, dst, small.at[n])
        for n, (src, dst) in enumerate((
            (pos_hbm, pos_ref), (band_hbm, band_ref), (fo_hbm, fo_ref), (so_hbm, so_ref),
            (ext_hbm, ext_ref),
            (win_hbm.at[:, pl.ds(pl.multiple_of(si * XW, XW), XW)], win_ref),
        ))
    ]
    for copy in smalls:
        copy.start()
    slab = d_ref.reshape(32, d_ref.shape[2])

    def own1(ch):
        return pltpu.make_async_copy(
            slab.at[:, pl.ds(pl.multiple_of(si * XW + ch * CW, CW), CW)],
            buf1.at[ch, pl.ds(pl.multiple_of(si * 32, 32), 32), :],
            loc.at[ch],
        )

    for ch in range(C):
        own1(ch).start()

    barrier = pltpu.get_barrier_semaphore()

    def greet(f, s):
        pl.semaphore_signal(barrier, inc=1, device_id=(f, s), device_id_type=MESH)

    def greet_sub(k, c):
        greet(fi, (si + k) & (NS - 1))
        return c

    def greet_facet(k, c):
        greet((fi + k) & (NF - 1), si)
        return c

    def greet_last(m, c):
        @pl.when(jnp.logical_not(jnp.logical_and(is_own4, m == m_own)))
        def _():
            greet(src4, 2 * m + jh)

        return c

    lax.fori_loop(1, NS, greet_sub, 0)
    lax.fori_loop(1, NF, greet_facet, 0)
    lax.fori_loop(0, NF, greet_last, 0)
    pl.semaphore_wait(barrier, NS - 1 + NF - 1 + NF - is_own4.astype(jnp.int32))

    for ch in range(C):

        def go1(k, c, ch=ch):
            to = (si + k) & (NS - 1)
            pltpu.make_async_remote_copy(
                src_ref=slab.at[:, pl.ds(pl.multiple_of(to * XW + ch * CW, CW), CW)],
                dst_ref=buf1.at[ch, pl.ds(pl.multiple_of(si * 32, 32), 32), :],
                send_sem=sends.at[0], recv_sem=r1.at[ch],
                device_id=(fi, to), device_id_type=MESH,
            ).start()
            return c

        lax.fori_loop(1, NS, go1, 0)

    for copy in smalls:
        copy.wait()

    band = band_ref[0]
    pos = pos_ref[...]
    pick = (iota((ROWS, 2 * ROWS), 1) >> 1 == iota((ROWS, 2 * ROWS), 0)).astype(BF16)
    digits = jnp.concatenate([pos >> 8, pos & 255], axis=0).astype(F32).astype(BF16)
    digits = jnp.dot(digits, pick, preferred_element_type=F32).astype(jnp.int32)
    twice = digits[0:1] * 256 + digits[1:2]
    turn = (iota((1, 2 * ROWS), 1) & 1) * 16384

    def row_table(g, c):
        cos, sin = cs(twice * (iota((8, 2 * ROWS), 0) + (8 * g + band)) - turn)
        high, low = split(jnp.concatenate([cos, -sin], axis=0))
        at = pl.ds(pl.multiple_of(16 * g, 16), 16)
        e_ref[0, at, :] = high
        e_ref[1, at, :] = low
        return c

    lax.fori_loop(0, 16, row_table, 0)

    lane = iota((1, 256), 1)
    off = jnp.zeros((1, 256), jnp.int32)
    for b in range(NF):
        off = jnp.where((lane >> 5) == b, fo_ref[b], off)

    def facet_table(g, c):
        row = iota((32, 256), 0)
        col = iota((32, 256), 1)
        cos, sin = cs(jnp.broadcast_to(off * (g * 8192), (32, 256)))
        rc, cc = (row >> 3) & 1, (col >> 3) & 1
        val = jnp.where(rc == cc, cos, jnp.where(rc == 0, sin, -sin))
        val = jnp.where(((row ^ col) & 0b10111) == 0, val, 0.0)
        fb[pl.ds(pl.multiple_of(32 * g, 32), 32), :] = val.astype(BF16)
        return c

    lax.fori_loop(0, NF, facet_table, 0)

    def first_freq(q):
        o = so_ref[q]
        return o + ((m_own - o) & 7)

    lane = iota((1, 128), 1)
    freq = jnp.zeros((1, 128), jnp.int32)
    for q in range(NF):
        freq = jnp.where(lane == q, first_freq(q), freq)

    def column_table(ac, c):
        step = 32
        a0 = ac * step
        base = cs((iota((step, NI), 0) + a0) * iota((step, NI), 1) * 8)
        ph = cs((iota((step, 128), 0) + a0) * freq)
        row = (ac // (CW // step)) * (2 * CW) + (ac % (CW // step)) * step
        top = pl.ds(pl.multiple_of(row, step), step)
        low = pl.ds(pl.multiple_of(row + CW, step), step)
        for q in range(NF):
            pq = (
                jnp.broadcast_to(ph[0][:, q : q + 1], (step, NI)),
                jnp.broadcast_to(ph[1][:, q : q + 1], (step, NI)),
            )
            cos, sin = cmul(base, pq)
            cos = cos.astype(BF16)
            sin = sin.astype(BF16)
            w_ref[q, top, pl.ds(0, NI)] = cos
            w_ref[q, top, pl.ds(NI, NI)] = -sin
            w_ref[q, low, pl.ds(0, NI)] = sin
            w_ref[q, low, pl.ds(NI, NI)] = cos
        return c

    lax.fori_loop(0, XW // 32, column_table, 0)

    fq = jnp.zeros((NF, NI), jnp.int32)
    for q in range(NF):
        fq = jnp.where(iota((NF, NI), 0) == q, first_freq(q), fq)
    fq = fq + 8 * iota((NF, NI), 1)
    z1 = cs(fq * 512)
    z2 = cs(fq * 1024)
    z_ref[0], z_ref[1] = z1[0], -z1[1]
    z_ref[2], z_ref[3] = z2[0], -z2[1]

    def sub_table(g, c):
        cos, sin = cs((iota((32, NI), 0) + 32 * g) * iota((32, NI), 1) * 256)
        at = pl.ds(pl.multiple_of(32 * g, 32), 32)
        for n, part in enumerate((cos, sin)):
            high, low = split(part)
            v_ref[0, at, pl.ds(n * NI, NI)] = high
            v_ref[1, at, pl.ds(n * NI, NI)] = low
        return c

    lax.fori_loop(0, 8, sub_table, 0)

    def wait(ref, sem):
        pltpu.make_async_copy(ref, ref, sem).wait()

    def rows(ch):
        own1(ch).wait()
        wait(buf1.at[ch, pl.ds(0, 480), :], r1.at[ch])
        data = buf1[ch]
        val = jnp.dot(e_ref[0], data, preferred_element_type=F32) + jnp.dot(
            e_ref[1], data, preferred_element_type=F32
        )
        send2[ch] = val.astype(BF16).reshape(NF, 32, CW)

        def go2(k, c):
            to = (fi + k) & (NF - 1)
            pltpu.make_async_remote_copy(
                src_ref=send2.at[ch, to], dst_ref=buf2.at[ch, fi],
                send_sem=sends.at[1], recv_sem=r2.at[ch],
                device_id=(to, si), device_id_type=MESH,
            ).start()
            return c

        lax.fori_loop(1, NF, go2, 0)
        buf2[ch, fi] = send2[ch, fi]

    def facets(ch):
        wait(buf2.at[ch, pl.ds(0, NF - 1)], r2.at[ch])
        summed = jnp.dot(fb[...], buf2[ch].reshape(256, CW), preferred_element_type=F32)
        val = summed * win_ref[:, pl.ds(ch * CW, CW)]
        send3[ch] = val.astype(BF16).reshape(NS, 16, CW)

        def go3(k, c):
            to = (si + k) & (NS - 1)
            pltpu.make_async_remote_copy(
                src_ref=send3.at[ch, to], dst_ref=buf3.at[ch, si],
                send_sem=sends.at[2], recv_sem=r3.at[ch],
                device_id=(fi, to), device_id_type=MESH,
            ).start()
            return c

        lax.fori_loop(1, NS, go3, 0)
        buf3[ch, si] = send3[ch, si]

    def gather(ch):
        wait(buf3.at[ch, pl.ds(0, NS - 1)], r3.at[ch])
        for t in range(8):
            one = buf3[ch, 2 * t].astype(F32)
            two = buf3[ch, 2 * t + 1].astype(F32)
            for c in range(2):
                part = jnp.concatenate([one[8 * c : 8 * c + 8], two[8 * c : 8 * c + 8]], axis=0)
                a_ref[pl.ds(16 * t, 16), pl.ds((2 * ch + c) * CW, CW)] = part.astype(BF16)

    steps = {"r": rows, "f": facets, "g": gather}
    for name, ch in ORDER:
        steps[name](ch)

    def copy4(q):
        return pltpu.make_async_remote_copy(
            src_ref=send4.at[q], dst_ref=buf4.at[m_own],
            send_sem=sends.at[3], recv_sem=r4,
            device_id=(q, dest4), device_id_type=MESH,
        )

    for n in range(NF):
        q = (fi + 1 + n) & (NF - 1)
        y = jnp.dot(a_ref[...], w_ref[q], preferred_element_type=F32)

        def part(e):
            return y[8 * e : 8 * e + 8, :NI], y[8 * e : 8 * e + 8, NI:]

        def row(i):
            return jnp.broadcast_to(z_ref[i, pl.ds(q, 1), :], (8, NI))

        zz = (row(2), row(3))
        even, odd = part(14), part(15)
        for e in range(12, -1, -2):
            even = cadd(cmul(even, zz), part(e))
            odd = cadd(cmul(odd, zz), part(e + 1))
        total = cadd(even, cmul(odd, (row(0), row(1))))
        k = ((m_own - so_ref[q]) & 7) + 8 * iota((8, NI), 1)
        keep = jnp.logical_and(k >= ext_ref[0, q], k < SG - ext_ref[1, q])
        both = jnp.concatenate(
            [jnp.where(keep, total[0], 0.0), jnp.where(keep, total[1], 0.0)], axis=0
        )
        send4[q] = both.astype(BF16)
        if n < NF - 1:
            copy4(q).start()
        else:
            @pl.when(is_own4)
            def _():
                buf4[m_own] = send4[q]

            @pl.when(jnp.logical_not(is_own4))
            def _():
                copy4(q).start()

    tw = cs(iota((NF, NI), 0) * iota((NF, NI), 1) * 32)
    wait(buf1.at[:, pl.ds(0, 480), :], sends.at[0])
    wait(buf2.at[:, pl.ds(0, NF - 1)], sends.at[1])
    wait(buf3.at[:, pl.ds(0, NS - 1)], sends.at[2])

    @pl.when(is_own4)
    def _():
        wait(buf4.at[pl.ds(0, NF - 1)], r4)

    @pl.when(jnp.logical_not(is_own4))
    def _():
        wait(buf4, r4)

    got = buf4[...].reshape(128, NI)
    spec = jnp.dot(got, v_ref[0], preferred_element_type=F32) + jnp.dot(
        got, v_ref[1], preferred_element_type=F32
    )
    for m in range(NF):
        re, im = spec[16 * m : 16 * m + 8], spec[16 * m + 8 : 16 * m + 16]
        tp_ref[m, 0] = re[:, :NI] - im[:, NI:]
        tp_ref[m, 1] = re[:, NI:] + im[:, :NI]
    own = so_ref[fi]
    terms = []
    for kap in range(NF):
        got = tp_ref[(own + kap) & 7]
        step = (
            jnp.broadcast_to(tw[0][kap : kap + 1], (8, NI)),
            jnp.broadcast_to(tw[1][kap : kap + 1], (8, NI)),
        )
        terms.append(cmul((got[0], got[1]), step))
    scale = 1.0 / (4096.0 * math.sqrt(SG))
    for n, val in enumerate(dft8(terms)):
        out_ref[0, :, pl.ds(n * NI, NI)] = val[0] * scale
        out_ref[1, :, pl.ds(n * NI, NI)] = val[1] * scale

    @pl.when(is_own4)
    def _():
        wait(buf4.at[pl.ds(0, NF - 1)], sends.at[3])

    @pl.when(jnp.logical_not(is_own4))
    def _():
        wait(buf4, sends.at[3])


def local(slab, window, facet_offsets, subgrid_offsets, row_positions, band_offset, extents):
    hbm = pl.BlockSpec(memory_space=pltpu.MemorySpace.HBM)
    dma = pltpu.SemaphoreType.DMA
    out = pl.pallas_call(
        kernel,
        out_shape=jax.ShapeDtypeStruct((2, 8, SG), F32),
        in_specs=[hbm] * 7,
        out_specs=pl.BlockSpec(memory_space=pltpu.VMEM),
        scratch_shapes=[
            pltpu.VMEM((1, XW), F32),
            pltpu.VMEM((1, ROWS), jnp.int32),
            pltpu.SMEM((NF,), jnp.int32),
            pltpu.SMEM((NF,), jnp.int32),
            pltpu.SMEM((1,), jnp.int32),
            pltpu.SMEM((2, NF), jnp.int32),
            pltpu.VMEM((C, 2 * ROWS, CW), BF16),
            pltpu.VMEM((2, ROWS, 2 * ROWS), BF16),
            pltpu.VMEM((C, NF, 32, CW), BF16),
            pltpu.VMEM((C, NF, 32, CW), BF16),
            pltpu.VMEM((256, 256), BF16),
            pltpu.VMEM((C, NS, 16, CW), BF16),
            pltpu.VMEM((C, NS, 16, CW), BF16),
            pltpu.VMEM((128, 2 * XW), BF16),
            pltpu.VMEM((NF, 2 * XW, 2 * NI), BF16),
            pltpu.VMEM((4, NF, NI), F32),
            pltpu.VMEM((NF, 16, NI), BF16),
            pltpu.VMEM((NF, 16, NI), BF16),
            pltpu.VMEM((2, NI, 2 * NI), BF16),
            pltpu.VMEM((NF, 2, 8, NI), F32),
            dma((4,)), dma((C,)), dma((C,)), dma((C,)), dma, dma((C,)), dma((6,)),
        ],
        compiler_params=pltpu.CompilerParams(
            collective_id=0, has_side_effects=True, vmem_limit_bytes=63 << 20
        ),
    )(
        slab, window.reshape(1, -1), row_positions.reshape(1, -1),
        facet_offsets, subgrid_offsets, band_offset, extents.T,
    )
    return out.transpose(1, 0, 2)[:, None]


def solution(mesh):
    return jax.shard_map(
        local,
        mesh=mesh,
        in_specs=(P("sub", None, "facet"), P(), P(), P(), P(), P(), P()),
        out_specs=P("sub", "facet", None, None),
        check_vma=False,
    )
```

time: 41.5 us -> 36.5 us (0.88)
  the two profiles are of different devices: /device:TPU:26 before, /device:TPU:2 now
where the time goes in v2:
time: 36.5 us; the launch traced here: 36.4 us
  Pallas kernels  34 us (93%)
  local copies, waits for them, and re-layouts  1.66 us (5%)
  between operations  0.66 us (2%)
    pallas_call x1, Pallas kernels, local(): pl.pallas_call(kernel, out_shape=jax.ShapeDtypeStruct((2, 8, SG), F32), i...  34 us
    broadcast_in_dim x1, local copies, waits for them, and re-layouts, local(): return out.transpose(1, 0, 2)[:, None]  1.66 us

profile of v2, /device:TPU:2, one launch (start us, length us, event | category | flops | bytes accessed | tf_op | source)
XLA Modules:
  0.0 36.4 jit_solution(15612147021641808019)
XLA Ops:
  0.7 34.0 %shard_map.73 = f32[2,8,2048]{2,1,0:T(8,128)} custom-call(bf16[16,2,8192]{2,1,0:T(2,128)(2,1)} %d_ref.1, f32[1,8192]{1,0:T(1,128)} %bitcast.7, s32[1,256]{1,0:T(1,128)} %bitcast.8, s32[8]{0:T(128)} %fo_hbm.1, s32[8]{0:T(128)} %so_hbm.1, s32[1]{0:T(128)S(6)} %copy.9.band_hbm, s32[2,8]{1,0:T(2,128)} %bitcast.9), custom_call_target="tpu_custom_call" | custom-call | tf_op jit(solution)/shard_map/pallas_call | solution.py:388
  34.7 1.7 %copy.8 = f32[8,1,2,2048]{3,2,1,0:T(2,128)} copy(f32[8,1,2,2048]{3,0,2,1:T(8,128)} %bitcast.6) | data formatting | bytes 262144 | tf_op jit(solution)/shard_map/broadcast_in_dim | solution.py:423

commit v3 on v2

--- a/solution.py
+++ b/solution.py
@@ -18,6 +18,7 @@
 SG = 2048
 C = 4
 CW = XW // C
+FAR = (True, True, True)
 ORDER = tuple((step, ch) for step in "rfg" for ch in range(C))
 
 
@@ -81,7 +82,7 @@
     d_ref, win_hbm, pos_hbm, fo_hbm, so_hbm, band_hbm, ext_hbm, out_ref,
     win_ref, pos_ref, fo_ref, so_ref, band_ref, ext_ref,
     buf1, e_ref, send2, buf2, fb, send3, buf3, a_ref, w_ref, z_ref, send4, buf4, v_ref, tp_ref,
-    sends, r1, r2, r3, r4, loc, small,
+    sends, r1, r2, r3, r4, loc, small, near, far,
 ):
     fi = lax.axis_index("facet")
     si = lax.axis_index("sub")
@@ -90,6 +91,27 @@
     dest4 = 2 * fi + jh
     src4 = si >> 1
     is_own4 = fi == src4
+
+    def sub_at(k):
+        code = k >> 2
+        x = ((si >> 1) + (code ^ (code >> 1))) & 3
+        return ((si >> 3) ^ ((k >> 1) & 1)) * 8 + x * 2 + ((si & 1) ^ (k & 1))
+
+    def facet_at(k):
+        code = k >> 1
+        return (((fi >> 1) + (code ^ (code >> 1))) & 3) * 2 + ((fi & 1) ^ (k & 1))
+
+    beside = (((fi + 2) & 7, si), ((fi + 6) & 7, si), (fi ^ 1, si))
+    barrier = pltpu.get_barrier_semaphore()
+
+    def greet(k, c):
+        to = sub_at(NS - k)
+        pl.semaphore_signal(barrier, inc=1, device_id=(fi, to), device_id_type=MESH)
+        return c
+
+    for to in beside:
+        pl.semaphore_signal(barrier, inc=1, device_id=to, device_id_type=MESH)
+    lax.fori_loop(1, NS, greet, 0)
 
     smalls = [
         pltpu.make_async_copy(src, dst, small.at[n])
@@ -113,35 +135,12 @@
     for ch in range(C):
         own1(ch).start()
 
-    barrier = pltpu.get_barrier_semaphore()
-
-    def greet(f, s):
-        pl.semaphore_signal(barrier, inc=1, device_id=(f, s), device_id_type=MESH)
-
-    def greet_sub(k, c):
-        greet(fi, (si + k) & (NS - 1))
-        return c
-
-    def greet_facet(k, c):
-        greet((fi + k) & (NF - 1), si)
-        return c
-
-    def greet_last(m, c):
-        @pl.when(jnp.logical_not(jnp.logical_and(is_own4, m == m_own)))
-        def _():
-            greet(src4, 2 * m + jh)
-
-        return c
-
-    lax.fori_loop(1, NS, greet_sub, 0)
-    lax.fori_loop(1, NF, greet_facet, 0)
-    lax.fori_loop(0, NF, greet_last, 0)
-    pl.semaphore_wait(barrier, NS - 1 + NF - 1 + NF - is_own4.astype(jnp.int32))
+    pl.semaphore_wait(barrier, NS - 1 + 3)
 
     for ch in range(C):
 
         def go1(k, c, ch=ch):
-            to = (si + k) & (NS - 1)
+            to = sub_at(NS - k if FAR[0] else k)
             pltpu.make_async_remote_copy(
                 src_ref=slab.at[:, pl.ds(pl.multiple_of(to * XW + ch * CW, CW), CW)],
                 dst_ref=buf1.at[ch, pl.ds(pl.multiple_of(si * 32, 32), 32), :],
@@ -151,6 +150,9 @@
             return c
 
         lax.fori_loop(1, NS, go1, 0)
+
+    for to in beside:
+        pl.semaphore_signal(near, inc=1, device_id=to, device_id_type=MESH)
 
     for copy in smalls:
         copy.wait()
@@ -189,6 +191,9 @@
         return c
 
     lax.fori_loop(0, NF, facet_table, 0)
+
+    pl.semaphore_wait(near, 3)
+    pl.semaphore_signal(far, inc=1, device_id=beside[1], device_id_type=MESH)
 
     def first_freq(q):
         o = so_ref[q]
@@ -242,6 +247,7 @@
         return c
 
     lax.fori_loop(0, 8, sub_table, 0)
+    pl.semaphore_wait(far, 1)
 
     def wait(ref, sem):
         pltpu.make_async_copy(ref, ref, sem).wait()
@@ -256,7 +262,7 @@
         send2[ch] = val.astype(BF16).reshape(NF, 32, CW)
 
         def go2(k, c):
-            to = (fi + k) & (NF - 1)
+            to = facet_at(NF - k if FAR[1] else k)
             pltpu.make_async_remote_copy(
                 src_ref=send2.at[ch, to], dst_ref=buf2.at[ch, fi],
                 send_sem=sends.at[1], recv_sem=r2.at[ch],
@@ -274,7 +280,7 @@
         send3[ch] = val.astype(BF16).reshape(NS, 16, CW)
 
         def go3(k, c):
-            to = (si + k) & (NS - 1)
+            to = sub_at(NS - k if FAR[2] else k)
             pltpu.make_async_remote_copy(
                 src_ref=send3.at[ch, to], dst_ref=buf3.at[ch, si],
                 send_sem=sends.at[2], recv_sem=r3.at[ch],
@@ -306,7 +312,7 @@
         )
 
     for n in range(NF):
-        q = (fi + 1 + n) & (NF - 1)
+        q = facet_at(NF - 1 - n)
         y = jnp.dot(a_ref[...], w_ref[q], preferred_element_type=F32)
 
         def part(e):
@@ -412,6 +418,7 @@
             pltpu.VMEM((2, NI, 2 * NI), BF16),
             pltpu.VMEM((NF, 2, 8, NI), F32),
             dma((4,)), dma((C,)), dma((C,)), dma((C,)), dma, dma((C,)), dma((6,)),
+            pltpu.SemaphoreType.REGULAR, pltpu.SemaphoreType.REGULAR,
         ],
         compiler_params=pltpu.CompilerParams(
             collective_id=0, has_side_effects=True, vmem_limit_bytes=63 << 20

time: 36.5 us -> 35.3 us (0.967)
  the two profiles are of different devices: /device:TPU:2 before, /device:TPU:1 now
where the time goes in v3:
time: 35.3 us; the launch traced here: 35.1 us
  Pallas kernels  32.8 us (93%)
  local copies, waits for them, and re-layouts  1.66 us (5%)
  between operations  0.66 us (2%)
    pallas_call x1, Pallas kernels, local(): pl.pallas_call(kernel, out_shape=jax.ShapeDtypeStruct((2, 8, SG), F32), i...  32.8 us
    broadcast_in_dim x1, local copies, waits for them, and re-layouts, local(): return out.transpose(1, 0, 2)[:, None]  1.66 us

profile of v3, /device:TPU:1, one launch (start us, length us, event | category | flops | bytes accessed | tf_op | source)
XLA Modules:
  0.0 35.1 jit_solution(11967876114809913924)
XLA Ops:
  0.7 32.8 %shard_map.73 = f32[2,8,2048]{2,1,0:T(8,128)} custom-call(bf16[16,2,8192]{2,1,0:T(2,128)(2,1)} %d_ref.1, f32[1,8192]{1,0:T(1,128)} %bitcast.7, s32[1,256]{1,0:T(1,128)} %bitcast.8, s32[8]{0:T(128)} %fo_hbm.1, s32[8]{0:T(128)} %so_hbm.1, s32[1]{0:T(128)S(6)} %copy.9.band_hbm, s32[2,8]{1,0:T(2,128)} %bitcast.9), custom_call_target="tpu_custom_call" | custom-call | tf_op jit(solution)/shard_map/pallas_call | solution.py:394
  33.5 1.7 %copy.8 = f32[8,1,2,2048]{3,2,1,0:T(2,128)} copy(f32[8,1,2,2048]{3,0,2,1:T(8,128)} %bitcast.6) | data formatting | bytes 262144 | tf_op jit(solution)/shard_map/broadcast_in_dim | solution.py:430

commit v4 on v3

--- a/solution.py
+++ b/solution.py
@@ -421,12 +421,15 @@
             pltpu.SemaphoreType.REGULAR, pltpu.SemaphoreType.REGULAR,
         ],
         compiler_params=pltpu.CompilerParams(
-            collective_id=0, has_side_effects=True, vmem_limit_bytes=63 << 20
+            collective_id=0, has_side_effects=True, vmem_limit_bytes=40 << 20
         ),
-    )(
-        slab, window.reshape(1, -1), row_positions.reshape(1, -1),
-        facet_offsets, subgrid_offsets, band_offset, extents.T,
-    )
+    )(*(
+        x if x.size == 1 else pltpu.with_memory_space_constraint(x, pltpu.MemorySpace.HBM)
+        for x in (
+            slab, window.reshape(1, -1), row_positions.reshape(1, -1),
+            facet_offsets, subgrid_offsets, band_offset, extents.T,
+        )
+    ))
     return out.transpose(1, 0, 2)[:, None]
 
 

time: 35.3 us -> 33.7 us (0.955)
  local copies, waits for them, and re-layouts: 1.66 us -> 0.76 us
  Pallas kernels: 32.8 us -> 32.2 us
    broadcast_in_dim x1, local copies, waits for them, and re-layouts: 1.66 us -> 0.76 us  [local(): return out.transpose(1, 0, 2)[:, None]]
    pallas_call x1, Pallas kernels: 32.8 us -> 32.2 us  [local(): pl.pallas_call(kernel, out_shape=jax.ShapeDtypeStruct((2, 8, SG), F32), i...]
where the time goes in v4:
time: 33.7 us; the launch traced here: 33.6 us
  Pallas kernels  32.2 us (96%)
  local copies, waits for them, and re-layouts  0.76 us (2%)
  between operations  0.66 us (2%)
    pallas_call x1, Pallas kernels, local(): pl.pallas_call(kernel, out_shape=jax.ShapeDtypeStruct((2, 8, SG), F32), i...  32.2 us
    broadcast_in_dim x1, local copies, waits for them, and re-layouts, local(): return out.transpose(1, 0, 2)[:, None]  0.76 us

profile of v4, /device:TPU:1, one launch (start us, length us, event | category | flops | bytes accessed | tf_op | source)
XLA Modules:
  0.0 33.6 jit_solution(606060579305871777)
XLA Ops:
  0.7 32.2 %shard_map.73 = f32[2,8,2048]{2,1,0:T(8,128)S(1)} custom-call(bf16[16,2,8192]{2,1,0:T(2,128)(2,1)} %d_ref.1, f32[1,8192]{1,0:T(1,128)} %bitcast.7, s32[1,256]{1,0:T(1,128)} %bitcast.8, s32[8]{0:T(128)} %fo_hbm.1, s32[8]{0:T(128)} %so_hbm.1, s32[1]{0:T(128)S(6)} %copy.9.band_hbm, s32[2,8]{1,0:T(2,128)} %bitcast.9), custom_call_target="tpu_custom_call" | custom-call | tf_op jit(solution)/shard_map/pallas_call | solution.py:394
  32.8 0.8 %copy.8 = f32[8,1,2,2048]{3,2,1,0:T(2,128)} copy(f32[8,1,2,2048]{3,0,2,1:T(8,128)S(1)} %bitcast.6) | data formatting | bytes 262144 | tf_op jit(solution)/shard_map/broadcast_in_dim | solution.py:433

commit v5 on v4

--- a/solution.py
+++ b/solution.py
@@ -16,9 +16,9 @@
 XW = 512
 NI = 256
 SG = 2048
+CUT = 2
 C = 4
 CW = XW // C
-FAR = (True, True, True)
 ORDER = tuple((step, ch) for step in "rfg" for ch in range(C))
 
 
@@ -80,17 +80,16 @@
 
 def kernel(
     d_ref, win_hbm, pos_hbm, fo_hbm, so_hbm, band_hbm, ext_hbm, out_ref,
-    win_ref, pos_ref, fo_ref, so_ref, band_ref, ext_ref,
+    win_lo, win_hi, pos_ref, fo_ref, so_ref, band_ref, ext_ref,
     buf1, e_ref, send2, buf2, fb, send3, buf3, a_ref, w_ref, z_ref, send4, buf4, v_ref, tp_ref,
-    sends, r1, r2, r3, r4, loc, small, near, far,
+    sends, r1, r2, r3, r4, loc, small, near, far, y_ref,
 ):
     fi = lax.axis_index("facet")
     si = lax.axis_index("sub")
-    m_own = si >> 1
-    jh = si & 1
+    m_own = si & 7
+    jh = si >> 3
     dest4 = 2 * fi + jh
-    src4 = si >> 1
-    is_own4 = fi == src4
+    is_own4 = dest4 == si
 
     def sub_at(k):
         code = k >> 2
@@ -109,8 +108,9 @@
         pl.semaphore_signal(barrier, inc=1, device_id=(fi, to), device_id_type=MESH)
         return c
 
-    for to in beside:
-        pl.semaphore_signal(barrier, inc=1, device_id=to, device_id_type=MESH)
+    for f, s in beside:
+        for to in ((f, s ^ 8), (f, s)):
+            pl.semaphore_signal(barrier, inc=1, device_id=to, device_id_type=MESH)
     lax.fori_loop(1, NS, greet, 0)
 
     smalls = [
@@ -118,7 +118,8 @@
         for n, (src, dst) in enumerate((
             (pos_hbm, pos_ref), (band_hbm, band_ref), (fo_hbm, fo_ref), (so_hbm, so_ref),
             (ext_hbm, ext_ref),
-            (win_hbm.at[:, pl.ds(pl.multiple_of(si * XW, XW), XW)], win_ref),
+            (win_hbm.at[:, pl.ds(pl.multiple_of(m_own * XW, XW), XW)], win_lo),
+            (win_hbm.at[:, pl.ds(pl.multiple_of((m_own + 8) * XW, XW), XW)], win_hi),
         ))
     ]
     for copy in smalls:
@@ -135,12 +136,12 @@
     for ch in range(C):
         own1(ch).start()
 
-    pl.semaphore_wait(barrier, NS - 1 + 3)
+    pl.semaphore_wait(barrier, NS - 1 + 6)
 
     for ch in range(C):
 
         def go1(k, c, ch=ch):
-            to = sub_at(NS - k if FAR[0] else k)
+            to = sub_at(NS - k)
             pltpu.make_async_remote_copy(
                 src_ref=slab.at[:, pl.ds(pl.multiple_of(to * XW + ch * CW, CW), CW)],
                 dst_ref=buf1.at[ch, pl.ds(pl.multiple_of(si * 32, 32), 32), :],
@@ -175,19 +176,19 @@
 
     lax.fori_loop(0, 16, row_table, 0)
 
-    lane = iota((1, 256), 1)
-    off = jnp.zeros((1, 256), jnp.int32)
+    lane = iota((1, 128), 1)
+    off = jnp.zeros((1, 128), jnp.int32)
     for b in range(NF):
-        off = jnp.where((lane >> 5) == b, fo_ref[b], off)
+        off = jnp.where((lane >> 4) == b, fo_ref[b], off)
 
     def facet_table(g, c):
-        row = iota((32, 256), 0)
-        col = iota((32, 256), 1)
-        cos, sin = cs(jnp.broadcast_to(off * (g * 8192), (32, 256)))
+        row = iota((16, 128), 0)
+        col = iota((16, 128), 1)
+        cos, sin = cs(jnp.broadcast_to(off * (g * 8192), (16, 128)))
         rc, cc = (row >> 3) & 1, (col >> 3) & 1
         val = jnp.where(rc == cc, cos, jnp.where(rc == 0, sin, -sin))
-        val = jnp.where(((row ^ col) & 0b10111) == 0, val, 0.0)
-        fb[pl.ds(pl.multiple_of(32 * g, 32), 32), :] = val.astype(BF16)
+        val = jnp.where(((row ^ col) & 0b111) == 0, val, 0.0)
+        fb[pl.ds(pl.multiple_of(16 * g, 16), 16), :] = val.astype(BF16)
         return c
 
     lax.fori_loop(0, NF, facet_table, 0)
@@ -259,43 +260,49 @@
         val = jnp.dot(e_ref[0], data, preferred_element_type=F32) + jnp.dot(
             e_ref[1], data, preferred_element_type=F32
         )
-        send2[ch] = val.astype(BF16).reshape(NF, 32, CW)
-
-        def go2(k, c):
-            to = facet_at(NF - k if FAR[1] else k)
+        send2[ch] = val.astype(BF16).reshape(NS, 16, CW)
+
+        def go2(n, c):
+            k = NS - n
+            f = facet_at(k >> 1)
+            half = jh ^ (k & 1)
             pltpu.make_async_remote_copy(
-                src_ref=send2.at[ch, to], dst_ref=buf2.at[ch, fi],
+                src_ref=send2.at[ch, 2 * f + half], dst_ref=buf2.at[ch, 8 * jh + fi],
                 send_sem=sends.at[1], recv_sem=r2.at[ch],
-                device_id=(to, si), device_id_type=MESH,
+                device_id=(f, 8 * half + m_own), device_id_type=MESH,
             ).start()
             return c
 
-        lax.fori_loop(1, NF, go2, 0)
-        buf2[ch, fi] = send2[ch, fi]
+        lax.fori_loop(1, NS, go2, 0)
+        buf2[ch, 8 * jh + fi] = send2[ch, dest4]
 
     def facets(ch):
-        wait(buf2.at[ch, pl.ds(0, NF - 1)], r2.at[ch])
-        summed = jnp.dot(fb[...], buf2[ch].reshape(256, CW), preferred_element_type=F32)
-        val = summed * win_ref[:, pl.ds(ch * CW, CW)]
-        send3[ch] = val.astype(BF16).reshape(NS, 16, CW)
-
-        def go3(k, c):
-            to = sub_at(NS - k if FAR[2] else k)
+        wait(buf2.at[ch, pl.ds(0, NS - 1)], r2.at[ch])
+        for half, win in enumerate((win_lo, win_hi)):
+            data = buf2[ch, pl.ds(8 * half, 8)].reshape(128, CW)
+            val = jnp.dot(fb[...], data, preferred_element_type=F32) * win[:, pl.ds(ch * CW, CW)]
+            send3[ch, :, half] = val.astype(BF16).reshape(NF, 16, CW)
+
+        def go3(n, c):
+            k = NF - n
+            code = k >> 1
+            x = ((m_own >> 1) + (code ^ (code >> 1))) & 3
+            to = 2 * x + ((m_own & 1) ^ (k & 1))
             pltpu.make_async_remote_copy(
-                src_ref=send3.at[ch, to], dst_ref=buf3.at[ch, si],
+                src_ref=send3.at[ch, to], dst_ref=buf3.at[ch, m_own],
                 send_sem=sends.at[2], recv_sem=r3.at[ch],
-                device_id=(fi, to), device_id_type=MESH,
+                device_id=(fi, 8 * jh + to), device_id_type=MESH,
             ).start()
             return c
 
-        lax.fori_loop(1, NS, go3, 0)
-        buf3[ch, si] = send3[ch, si]
+        lax.fori_loop(1, NF, go3, 0)
+        buf3[ch, m_own] = send3[ch, m_own]
 
     def gather(ch):
-        wait(buf3.at[ch, pl.ds(0, NS - 1)], r3.at[ch])
+        wait(buf3.at[ch, pl.ds(0, NF - 1)], r3.at[ch])
         for t in range(8):
-            one = buf3[ch, 2 * t].astype(F32)
-            two = buf3[ch, 2 * t + 1].astype(F32)
+            one = buf3[ch, (2 * t) % 8, t // 4].astype(F32)
+            two = buf3[ch, (2 * t + 1) % 8, t // 4].astype(F32)
             for c in range(2):
                 part = jnp.concatenate([one[8 * c : 8 * c + 8], two[8 * c : 8 * c + 8]], axis=0)
                 a_ref[pl.ds(16 * t, 16), pl.ds((2 * ch + c) * CW, CW)] = part.astype(BF16)
@@ -303,6 +310,12 @@
     steps = {"r": rows, "f": facets, "g": gather}
     for name, ch in ORDER:
         steps[name](ch)
+        if (name, ch) == ("g", CUT - 1):
+            for n in range(NF):
+                y_ref[n] = jnp.dot(
+                    a_ref[:, : 2 * CUT * CW], w_ref[facet_at(NF - 1 - n), : 2 * CUT * CW, :],
+                    preferred_element_type=F32,
+                )
 
     def copy4(q):
         return pltpu.make_async_remote_copy(
@@ -313,7 +326,9 @@
 
     for n in range(NF):
         q = facet_at(NF - 1 - n)
-        y = jnp.dot(a_ref[...], w_ref[q], preferred_element_type=F32)
+        y = y_ref[n] + jnp.dot(
+            a_ref[:, 2 * CUT * CW :], w_ref[q, 2 * CUT * CW :, :], preferred_element_type=F32
+        )
 
         def part(e):
             return y[8 * e : 8 * e + 8, :NI], y[8 * e : 8 * e + 8, NI:]
@@ -346,8 +361,8 @@
 
     tw = cs(iota((NF, NI), 0) * iota((NF, NI), 1) * 32)
     wait(buf1.at[:, pl.ds(0, 480), :], sends.at[0])
-    wait(buf2.at[:, pl.ds(0, NF - 1)], sends.at[1])
-    wait(buf3.at[:, pl.ds(0, NS - 1)], sends.at[2])
+    wait(buf2.at[:, pl.ds(0, NS - 1)], sends.at[1])
+    wait(buf3.at[:, pl.ds(0, NF - 1)], sends.at[2])
 
     @pl.when(is_own4)
     def _():
@@ -398,6 +413,7 @@
         out_specs=pl.BlockSpec(memory_space=pltpu.VMEM),
         scratch_shapes=[
             pltpu.VMEM((1, XW), F32),
+            pltpu.VMEM((1, XW), F32),
             pltpu.VMEM((1, ROWS), jnp.int32),
             pltpu.SMEM((NF,), jnp.int32),
             pltpu.SMEM((NF,), jnp.int32),
@@ -405,11 +421,11 @@
             pltpu.SMEM((2, NF), jnp.int32),
             pltpu.VMEM((C, 2 * ROWS, CW), BF16),
             pltpu.VMEM((2, ROWS, 2 * ROWS), BF16),
-            pltpu.VMEM((C, NF, 32, CW), BF16),
-            pltpu.VMEM((C, NF, 32, CW), BF16),
-            pltpu.VMEM((256, 256), BF16),
             pltpu.VMEM((C, NS, 16, CW), BF16),
             pltpu.VMEM((C, NS, 16, CW), BF16),
+            pltpu.VMEM((128, 128), BF16),
+            pltpu.VMEM((C, NF, 2, 16, CW), BF16),
+            pltpu.VMEM((C, NF, 2, 16, CW), BF16),
             pltpu.VMEM((128, 2 * XW), BF16),
             pltpu.VMEM((NF, 2 * XW, 2 * NI), BF16),
             pltpu.VMEM((4, NF, NI), F32),
@@ -417,8 +433,9 @@
             pltpu.VMEM((NF, 16, NI), BF16),
             pltpu.VMEM((2, NI, 2 * NI), BF16),
             pltpu.VMEM((NF, 2, 8, NI), F32),
-            dma((4,)), dma((C,)), dma((C,)), dma((C,)), dma, dma((C,)), dma((6,)),
+            dma((4,)), dma((C,)), dma((C,)), dma((C,)), dma, dma((C,)), dma((7,)),
             pltpu.SemaphoreType.REGULAR, pltpu.SemaphoreType.REGULAR,
+            pltpu.VMEM((NF, 128, 2 * NI), F32),
         ],
         compiler_params=pltpu.CompilerParams(
             collective_id=0, has_side_effects=True, vmem_limit_bytes=40 << 20

time: 33.7 us -> 33.3 us (0.988)
  Pallas kernels: 32.2 us -> 31.8 us
    pallas_call x1, Pallas kernels: 32.2 us -> 31.8 us  [local(): pl.pallas_call(kernel, out_shape=jax.ShapeDtypeStruct((2, 8, SG), F32), i...]
where the time goes in v5:
time: 33.3 us; the launch traced here: 33.2 us
  Pallas kernels  31.8 us (95%)
  local copies, waits for them, and re-layouts  0.76 us (2%)
  between operations  0.66 us (2%)
    pallas_call x1, Pallas kernels, local(): pl.pallas_call(kernel, out_shape=jax.ShapeDtypeStruct((2, 8, SG), F32), i...  31.8 us
    broadcast_in_dim x1, local copies, waits for them, and re-layouts, local(): return out.transpose(1, 0, 2)[:, None]  0.76 us

profile of v5, /device:TPU:1, one launch (start us, length us, event | category | flops | bytes accessed | tf_op | source)
XLA Modules:
  0.0 33.2 jit_solution(3456533391243108224)
XLA Ops:
  0.7 31.8 %shard_map.73 = f32[2,8,2048]{2,1,0:T(8,128)S(1)} custom-call(bf16[16,2,8192]{2,1,0:T(2,128)(2,1)} %d_ref.1, f32[1,8192]{1,0:T(1,128)} %bitcast.7, s32[1,256]{1,0:T(1,128)} %bitcast.8, s32[8]{0:T(128)} %fo_hbm.1, s32[8]{0:T(128)} %so_hbm.1, s32[1]{0:T(128)S(6)} %copy.9.band_hbm, s32[2,8]{1,0:T(2,128)} %bitcast.9), custom_call_target="tpu_custom_call" | custom-call | tf_op jit(solution)/shard_map/pallas_call | solution.py:409
  32.5 0.8 %copy.8 = f32[8,1,2,2048]{3,2,1,0:T(2,128)} copy(f32[8,1,2,2048]{3,0,2,1:T(8,128)S(1)} %bitcast.6) | data formatting | bytes 262144 | tf_op jit(solution)/shard_map/broadcast_in_dim | solution.py:450

commit v6 on v5

--- a/solution.py
+++ b/solution.py
@@ -82,7 +82,7 @@
     d_ref, win_hbm, pos_hbm, fo_hbm, so_hbm, band_hbm, ext_hbm, out_ref,
     win_lo, win_hi, pos_ref, fo_ref, so_ref, band_ref, ext_ref,
     buf1, e_ref, send2, buf2, fb, send3, buf3, a_ref, w_ref, z_ref, send4, buf4, v_ref, tp_ref,
-    sends, r1, r2, r3, r4, loc, small, near, far, y_ref,
+    sends, r1, r2, r3, r4, loc, small, near, far, y_ref, slab,
 ):
     fi = lax.axis_index("facet")
     si = lax.axis_index("sub")
@@ -124,7 +124,8 @@
     ]
     for copy in smalls:
         copy.start()
-    slab = d_ref.reshape(32, d_ref.shape[2])
+    staged = pltpu.make_async_copy(d_ref.reshape(32, d_ref.shape[2]), slab, small.at[7])
+    staged.start()
 
     def own1(ch):
         return pltpu.make_async_copy(
@@ -133,10 +134,12 @@
             loc.at[ch],
         )
 
+
+    pl.semaphore_wait(barrier, NS - 1 + 6)
+
+    staged.wait()
     for ch in range(C):
         own1(ch).start()
-
-    pl.semaphore_wait(barrier, NS - 1 + 6)
 
     for ch in range(C):
 
@@ -433,9 +436,10 @@
             pltpu.VMEM((NF, 16, NI), BF16),
             pltpu.VMEM((2, NI, 2 * NI), BF16),
             pltpu.VMEM((NF, 2, 8, NI), F32),
-            dma((4,)), dma((C,)), dma((C,)), dma((C,)), dma, dma((C,)), dma((7,)),
+            dma((4,)), dma((C,)), dma((C,)), dma((C,)), dma, dma((C,)), dma((8,)),
             pltpu.SemaphoreType.REGULAR, pltpu.SemaphoreType.REGULAR,
             pltpu.VMEM((NF, 128, 2 * NI), F32),
+            pltpu.VMEM((32, slab.shape[2]), BF16),
         ],
         compiler_params=pltpu.CompilerParams(
             collective_id=0, has_side_effects=True, vmem_limit_bytes=40 << 20

time: 33.3 us -> 33.2 us (level)
  no operation moved by 1% of the time
where the time goes in v6:
time: 33.2 us; the launch traced here: 33.1 us
  Pallas kernels  31.7 us (95%)
  local copies, waits for them, and re-layouts  0.76 us (2%)
  between operations  0.66 us (2%)
    pallas_call x1, Pallas kernels, local(): pl.pallas_call(kernel, out_shape=jax.ShapeDtypeStruct((2, 8, SG), F32), i...  31.7 us
    broadcast_in_dim x1, local copies, waits for them, and re-layouts, local(): return out.transpose(1, 0, 2)[:, None]  0.76 us

profile of v6, /device:TPU:1, one launch (start us, length us, event | category | flops | bytes accessed | tf_op | source)
XLA Modules:
  0.0 33.1 jit_solution(4580093326555874575)
XLA Ops:
  0.7 31.7 %shard_map.73 = f32[2,8,2048]{2,1,0:T(8,128)S(1)} custom-call(bf16[16,2,8192]{2,1,0:T(2,128)(2,1)} %d_ref.1, f32[1,8192]{1,0:T(1,128)} %bitcast.7, s32[1,256]{1,0:T(1,128)} %bitcast.8, s32[8]{0:T(128)} %fo_hbm.1, s32[8]{0:T(128)} %so_hbm.1, s32[1]{0:T(128)S(6)} %copy.9.band_hbm, s32[2,8]{1,0:T(2,128)} %bitcast.9), custom_call_target="tpu_custom_call" | custom-call | tf_op jit(solution)/shard_map/pallas_call | solution.py:412
  32.3 0.8 %copy.8 = f32[8,1,2,2048]{3,2,1,0:T(2,128)} copy(f32[8,1,2,2048]{3,0,2,1:T(8,128)S(1)} %bitcast.6) | data formatting | bytes 262144 | tf_op jit(solution)/shard_map/broadcast_in_dim | solution.py:454

commit v7 on v6

--- a/solution.py
+++ b/solution.py
@@ -91,6 +91,9 @@
     dest4 = 2 * fi + jh
     is_own4 = dest4 == si
 
+    staged = pltpu.make_async_copy(d_ref.reshape(32, d_ref.shape[2]), slab, small.at[7])
+    staged.start()
+
     def sub_at(k):
         code = k >> 2
         x = ((si >> 1) + (code ^ (code >> 1))) & 3
@@ -124,8 +127,6 @@
     ]
     for copy in smalls:
         copy.start()
-    staged = pltpu.make_async_copy(d_ref.reshape(32, d_ref.shape[2]), slab, small.at[7])
-    staged.start()
 
     def own1(ch):
         return pltpu.make_async_copy(

time: 33.2 us -> 33.2 us (level)
  no operation moved by 1% of the time
where the time goes in v7:
time: 33.2 us; the launch traced here: 33.1 us
  Pallas kernels  31.7 us (95%)
  local copies, waits for them, and re-layouts  0.76 us (2%)
  between operations  0.66 us (2%)
    pallas_call x1, Pallas kernels, local(): pl.pallas_call(kernel, out_shape=jax.ShapeDtypeStruct((2, 8, SG), F32), i...  31.7 us
    broadcast_in_dim x1, local copies, waits for them, and re-layouts, local(): return out.transpose(1, 0, 2)[:, None]  0.76 us

profile of v7, /device:TPU:1, one launch (start us, length us, event | category | flops | bytes accessed | tf_op | source)
XLA Modules:
  0.0 33.1 jit_solution(8949673669197536363)
XLA Ops:
  0.7 31.7 %shard_map.73 = f32[2,8,2048]{2,1,0:T(8,128)S(1)} custom-call(bf16[16,2,8192]{2,1,0:T(2,128)(2,1)} %d_ref.1, f32[1,8192]{1,0:T(1,128)} %bitcast.7, s32[1,256]{1,0:T(1,128)} %bitcast.8, s32[8]{0:T(128)} %fo_hbm.1, s32[8]{0:T(128)} %so_hbm.1, s32[1]{0:T(128)S(6)} %copy.9.band_hbm, s32[2,8]{1,0:T(2,128)} %bitcast.9), custom_call_target="tpu_custom_call" | custom-call | tf_op jit(solution)/shard_map/pallas_call | solution.py:413
  32.3 0.8 %copy.8 = f32[8,1,2,2048]{3,2,1,0:T(2,128)} copy(f32[8,1,2,2048]{3,0,2,1:T(8,128)S(1)} %bitcast.6) | data formatting | bytes 262144 | tf_op jit(solution)/shard_map/broadcast_in_dim | solution.py:455
